TPU v7x, 512 devices: a whole 4x8x8 slice. The times are simulated.
512 devices in a mesh: clip: 64 (over z, y_hi, x), val: 8 (over y_lo, core).
Axes of the slice: x: 4, y: 8 (y_hi: 2, y_lo: 4; y = y_hi * 4 + y_lo), z: 8, core: 2. Of those that a mesh axis runs over, the one named last changes fastest.
Arguments:
- latents: bfloat16 [1024, 8192], P('clip', 'val'), may hold values from -10 to 10
- noise: bfloat16 [1024, 8192], P('clip', 'val'), may hold values from -10 to 10
- offsets: int32 [1024, 2, 2], P('clip'), may hold values from 0 to 15
- times: float32 [1024], P('clip'), may hold values from 0.05 to 0.95
- embed: bfloat16 [64, 5120], replicated, may hold values from -0.75 to 0.75
Outputs:
- embedded: bfloat16 [1024, 128, 5120], P('clip', 'val')
All inputs are finite; a program needn't handle non-finite values.
Results may differ from a plain program's by a relative error of at most 0.0051.
Values may be sent and summed in bfloat16 or wider, within the bound.
A program may use at most 64 MiB of HBM per device.

v0:
```python
import math

import jax
import jax.numpy as jnp
from jax import lax
from jax.sharding import PartitionSpec as P

P_SIZE = 64
FR = 2
GW = 16
GH = 4
ITERS = 4
S = 128


def warp_noise(noise, offsets):
    clips = noise.shape[0]
    tokens = FR * GH * GW
    value_cube = noise.reshape(clips, noise.shape[1] // tokens, tokens)
    shift_y = offsets[:, :, 0] % GH
    shift_x = offsets[:, :, 1] % GW
    src_rows = (jnp.arange(GH, dtype=jnp.int32)[None, None, :] - shift_y[:, :, None]) % GH
    src_cols = (jnp.arange(GW, dtype=jnp.int32)[None, None, :] - shift_x[:, :, None]) % GW
    frame_base = (jnp.arange(FR, dtype=jnp.int32) * (GH * GW))[None, :, None, None]
    source = (frame_base + src_rows[:, :, :, None] * GW + src_cols[:, :, None, :]).reshape(
        clips, tokens
    )
    source = jnp.broadcast_to(source[:, None, :], value_cube.shape)
    return jnp.take_along_axis(value_cube, source, axis=2).reshape(noise.shape)


def row_stats(scores):
    top = jnp.max(scores, axis=1)
    total = jnp.sum(jnp.exp(scores - top[:, None]), axis=1)
    return (top, total)


def column_lse(scores):
    top = jnp.max(scores, axis=0)
    top = lax.pmax(top, "clip")
    total = lax.psum(jnp.sum(jnp.exp(scores - top[None, :]), axis=0), "clip")
    return top + jnp.log(total)


def on_device(latents, noise, offsets, times, embed):
    warped = warp_noise(noise, offsets)
    clips = latents.shape[0]
    volume = P_SIZE * S
    entropy = 0.5 / math.sqrt(volume)
    contract = (((1,), (1,)), ((), ()))
    panel_all = lax.all_gather(warped, "clip", axis=0, tiled=True)
    gram_part = lax.dot_general(latents, panel_all, contract, preferred_element_type=jnp.float32)
    square_part = jnp.sum(jnp.square(panel_all.astype(jnp.float32)), axis=1)
    gram, square = lax.psum((gram_part, square_part), "val")
    cost = (square[None, :] - 2.0 * gram) / volume
    column_dual = jnp.zeros((cost.shape[1],), jnp.float32)
    for sweep_index in range(ITERS):
        top, total = row_stats((column_dual[None, :] - cost) / entropy)
        row_dual = -entropy * (top + jnp.log(total))
        column_dual = -entropy * column_lse((row_dual[:, None] - cost) / entropy)
    scores = (column_dual[None, :] - cost) / entropy
    top, total = row_stats(scores)
    weights = (jnp.exp(scores - top[:, None]) / total[:, None]).astype(jnp.bfloat16)
    coupled = jnp.dot(weights, panel_all, preferred_element_type=jnp.float32)
    mixed = (
        (1.0 - times)[:, None] * latents.astype(jnp.float32) + times[:, None] * coupled
    ).astype(jnp.bfloat16)
    value_cube = mixed.reshape(clips, latents.shape[1] // S, S)
    return jnp.einsum(
        "cps,pd->csd",
        lax.all_to_all(value_cube, "val", split_axis=2, concat_axis=1, tiled=True),
        embed,
        preferred_element_type=jnp.float32,
    ).astype(jnp.bfloat16)


def solution(mesh):
    placed = (P("clip", "val"), P("clip", "val"), P("clip", None, None), P("clip"), P())
    return jax.shard_map(
        on_device, mesh=mesh, in_specs=placed, out_specs=P("clip", "val", None), check_vma=False
    )
```

profile of v0, /device:TPU:1, one launch (start us, length us, event | category | flops | bytes accessed | tf_op | source)
XLA Modules:
  0.0 2139.3 jit_solution(8296339982809576350)
XLA Ops:
  8.7 145.1 %gather_fusion = bf16[16384]{0:T(1024)(128)(2,1)S(1)} fusion(bf16[16,8,128]{2,1,0:T(8,128)(2,1)S(1)} %bitcast.32, s32[16384]{0:T(1024)S(1)} %or_bitcast_fusion), kind=kCustom, calls=%fused_computation | custom fusion | bytes 262144 | tf_op jit(solution)/shard_map/jit(take_along_axis)/gather | solution.py:29
  154.6 135.1 %all-gather.2.cloned.1.call-done = bf16[1024,1024]{1,0:T(8,128)(2,1)} async-done(((bf16[16,1024]{1,0:T(8,128)(2,1)}), bf16[1024,1024]{1,0:T(8,128)(2,1)}) %all-gather.2.cloned.1.call-update) | async-done | bytes 2097168 | tf_op jit(solution)/shard_map/all_gather | solution.py:51
  289.7 3.0 convolution_bitcast_fusion
  293.3 17.5 psum.42
  310.8 55.7 %all-reduce.2.cloned.1.call-done = f32[16,1024]{1,0:T(8,128)} async-done(((f32[16,1024]{1,0:T(8,128)}), f32[16,1024]{1,0:T(8,128)}) %all-reduce.2.cloned.1.call-update) | async-done | bytes 65552 | tf_op jit(solution)/shard_map/psum | solution.py:54
  366.5 1.0 fusion.7
  367.5 1.0 exponential_reduce_fusion.7
  368.5 0.9 fusion.8
  369.4 197.3 %pmax.28 = f32[1024]{0:T(1024)S(1)} all-reduce(f32[1024]{0:T(1024)S(1)} %fusion.8), channel_id=1, replica_groups=mesh['clip'=64,'val'=8] {'clip'}, use_global_device_ids=true, to_apply=%region_6.7 | all-reduce | flops 1024 | bytes 8192 | tf_op jit(solution)/shard_map/pmax | solution.py:40
  566.7 0.9 exponential_reduce_fusion.6
  567.6 187.5 %psum.44 = f32[1024]{0:T(1024)S(1)} all-reduce(f32[1024]{0:T(1024)S(1)} %exponential_reduce_fusion.6), channel_id=1, replica_groups=mesh['clip'=64,'val'=8] {'clip'}, use_global_device_ids=true, to_apply=%region_8.9 | all-reduce | flops 1024 | bytes 8192 | tf_op jit(solution)/shard_map/psum | solution.py:41
  755.2 1.0 fusion.9
  756.1 1.0 exponential_reduce_fusion.5
  757.2 0.9 fusion.10
  758.1 188.7 %pmax.29 = f32[1024]{0:T(1024)S(1)} all-reduce(f32[1024]{0:T(1024)S(1)} %fusion.10), channel_id=1, replica_groups=mesh['clip'=64,'val'=8] {'clip'}, use_global_device_ids=true, to_apply=%region_12.13 | all-reduce | flops 1024 | bytes 8192 | tf_op jit(solution)/shard_map/pmax | solution.py:40
  946.8 0.9 exponential_reduce_fusion.4
  947.8 187.4 %psum.45 = f32[1024]{0:T(1024)S(1)} all-reduce(f32[1024]{0:T(1024)S(1)} %exponential_reduce_fusion.4), channel_id=1, replica_groups=mesh['clip'=64,'val'=8] {'clip'}, use_global_device_ids=true, to_apply=%region_14.15 | all-reduce | flops 1024 | bytes 8192 | tf_op jit(solution)/shard_map/psum | solution.py:41
  1135.1 1.0 fusion.11
  1136.1 1.0 exponential_reduce_fusion.3
  1138.1 189.1 %pmax.30 = f32[1024]{0:T(1024)S(1)} all-reduce(f32[1024]{0:T(1024)S(1)} %fusion.12), channel_id=1, replica_groups=mesh['clip'=64,'val'=8] {'clip'}, use_global_device_ids=true, to_apply=%region_18.19 | all-reduce | flops 1024 | bytes 8192 | tf_op jit(solution)/shard_map/pmax | solution.py:40
  1327.2 0.9 exponential_reduce_fusion.2
  1328.2 187.5 %psum.46 = f32[1024]{0:T(1024)S(1)} all-reduce(f32[1024]{0:T(1024)S(1)} %exponential_reduce_fusion.2), channel_id=1, replica_groups=mesh['clip'=64,'val'=8] {'clip'}, use_global_device_ids=true, to_apply=%region_20.21 | all-reduce | flops 1024 | bytes 8192 | tf_op jit(solution)/shard_map/psum | solution.py:41
  1515.7 1.0 fusion.13
  1516.7 1.0 exponential_reduce_fusion.1
  1518.7 189.0 %pmax.31 = f32[1024]{0:T(1024)S(1)} all-reduce(f32[1024]{0:T(1024)S(1)} %fusion.14), channel_id=1, replica_groups=mesh['clip'=64,'val'=8] {'clip'}, use_global_device_ids=true, to_apply=%region_24.25 | all-reduce | flops 1024 | bytes 8192 | tf_op jit(solution)/shard_map/pmax | solution.py:40
  1707.7 0.9 exponential_reduce_fusion
  1708.6 187.5 %psum.47 = f32[1024]{0:T(1024)S(1)} all-reduce(f32[1024]{0:T(1024)S(1)} %exponential_reduce_fusion), channel_id=1, replica_groups=mesh['clip'=64,'val'=8] {'clip'}, use_global_device_ids=true, to_apply=%region_26.27 | all-reduce | flops 1024 | bytes 8192 | tf_op jit(solution)/shard_map/psum | solution.py:41
  1896.1 1.0 fusion.15
  1897.1 1.0 fusion.16
  1898.1 1.3 fusion.2
  1899.9 229.7 %all_to_all.18 = bf16[8,2,1024]{2,1,0:T(2,128)(2,1)S(1)} all-to-all(bf16[8,2,1024]{2,1,0:T(2,128)(2,1)S(1)} %reshape.134), channel_id=1, replica_groups=mesh['clip'=64,'val'=8] {'val'}, dimensions={0} | all-to-all | bytes 65536 | tf_op jit(solution)/shard_map/all_to_all | solution.py:71
  2130.3 2.1 convolution_convert_fusion
  (43 shorter events, 6.6 us)
Async XLA Ops:
  6.5 2123.8 %copy-start = (bf16[64,5120]{1,0:T(8,128)(2,1)S(1)}, bf16[64,5120]{1,0:T(8,128)(2,1)}, u32[]{:S(2)}) copy-start(bf16[64,5120]{1,0:T(8,128)(2,1)} %param.9) | copy-start | bytes 1966084
  6.5 283.2 %all-gather.2.cloned.1.call-start = ((), (), s32[]{:S(2)}) async-start(), calls=%async_computation.1 | async-start | bytes 2129920 | tf_op jit(solution)/shard_map/all_gather | solution.py:51
  8.7 145.9 %copy-start.3 = (f32[16]{0:T(128)S(1)}, f32[16]{0:T(128)}, u32[]{:S(2)}) copy-start(f32[16]{0:T(128)} %param.8) | copy-start | bytes 196
  8.7 281.0 %copy-start.2 = (bf16[16,1024]{1,0:T(8,128)(2,1)S(1)}, bf16[16,1024]{1,0:T(8,128)(2,1)}, u32[]{:S(2)}) copy-start(bf16[16,1024]{1,0:T(8,128)(2,1)} %param.5) | copy-start | bytes 98308
  154.5 212.0 %all-reduce.2.cloned.1.call-start = ((), (), s32[]{:S(2)}) async-start(), calls=%async_computation.2 | async-start | bytes 131072 | tf_op jit(solution)/shard_map/psum | solution.py:54
  289.7 3.1 copy-start.1
Sparse Core Ops, SparseCore 0:
  154.7 135.0 all-gather.1
  292.9 73.5 all-reduce.1
where the time goes:
time: 2140 us
  blocking collectives  1760 us (82%)
  waiting for transfers between devices  191 us (9%)
  local copies, waits for them, and re-layouts  148 us (7%)
    pmax x4, blocking collectives, column_lse(): top = lax.pmax(top, 'clip')  764 us
    psum x4, blocking collectives, column_lse(): total = lax.psum(jnp.sum(jnp.exp(scores - top[None, :]), axis=0), 'clip')  750 us
    all_to_all x1, blocking collectives, on_device(): lax.all_to_all(value_cube, 'val', split_axis=2, concat_axis=1, tiled=True)  230 us
    gather x1, local copies, waits for them, and re-layouts, warp_noise(): return jnp.take_along_axis(value_cube, source, axis=2).reshape(noise.shape)  145 us
    all_gather x1, waiting for transfers between devices, on_device(): panel_all = lax.all_gather(warped, 'clip', axis=0, tiled=True)  135 us
    psum x1, waiting for transfers between devices, on_device(): gram, square = lax.psum((gram_part, square_part), 'val')  55.7 us
  transfers between devices with their start and end apart: 2, of which 2 were waited for; matrix products, arithmetic and copies ran while one was open for 0% of the time, Pallas kernels for 0%

commit v1 on v0

v1 whole, which is shorter than its diff:
```python
import functools
import math

import jax
import jax.numpy as jnp
from jax import lax
from jax.experimental import pallas as pl
from jax.experimental.pallas import tpu as pltpu
from jax.sharding import PartitionSpec as P

P_SIZE = 64
FR = 2
GW = 16
GH = 4
ITERS = 4
S = FR * GH * GW
LOG2E = 1.4426950408889634


def each(n, step):
    def body(i, carry):
        step(i)
        return carry

    lax.fori_loop(1, n, body, 0)


def couple(nz, nb, nv, lat, noise, off, times, out, wg, lg, part, rv, g, ex, urow, pf, pb, rp, mt, ra,
           w_s, w_r, l_s, l_r, r_s, r_r, g_s, g_r, h_s, h_r, e_s, e_r, c_s, c_r, a_s, a_r):
    nl = nv // 2
    rows, depth = lat.shape
    patches = depth // S
    wide = nz * rows
    st = S // nv
    clip = lax.axis_index("clip")
    v = lax.axis_index("val")
    z, b = clip // nb, lax.rem(clip, nb)
    l, k = v // 2, lax.rem(v, 2)

    def slot(i):
        return lax.rem(i, 2) * nl + i // 2

    def at(z_, b_, v_):
        return {"clip": z_ * nb + b_, "val": v_}

    def along_z(i):
        return at(lax.rem(z + i, nz), b, v)

    def along_b(i):
        return at(z, lax.rem(b + i, nb), v)

    def along_v(i):
        return at(z, b, lax.rem(v + i, nv))

    def send(src, dst, s_sem, r_sem, where):
        return pltpu.make_async_remote_copy(src, dst, s_sem, r_sem, device_id=where)

    barrier = pltpu.get_barrier_semaphore()
    each(nz, lambda i: pl.semaphore_signal(barrier, inc=1, device_id=along_z(i)))
    each(nb, lambda i: pl.semaphore_signal(barrier, inc=1, device_id=along_b(i)))
    each(nv, lambda i: pl.semaphore_signal(barrier, inc=1, device_id=along_v(i)))

    rowi = lax.broadcasted_iota(jnp.int32, (rows, S), 0)
    lane = lax.broadcasted_iota(jnp.int32, (rows, S), 1)
    first = lane < GH * GW
    sy = jnp.zeros((rows, S), jnp.int32)
    sx = jnp.zeros((rows, S), jnp.int32)
    tv = jnp.zeros((rows, S), jnp.float32)
    for i in range(rows):
        here = rowi == i
        sy = jnp.where(here, jnp.where(first, off[i, 0], off[i, 2]), sy)
        sx = jnp.where(here, jnp.where(first, off[i, 1], off[i, 3]), sx)
        tv = jnp.where(here, times[i], tv)
    col = lane & (GW - 1)
    row = (lane // GW) & (GH - 1)
    for p in range(patches):
        x = noise[:, p * S:(p + 1) * S].astype(jnp.float32)
        for bit in (1, 2, 4, 8):
            turned = jnp.where(col >= bit, pltpu.roll(x, bit, 1), pltpu.roll(x, S - GW + bit, 1))
            x = jnp.where((sx & bit) != 0, turned, x)
        for bit in (1, 2):
            turned = jnp.where(
                row >= bit, pltpu.roll(x, bit * GW, 1), pltpu.roll(x, S - GH * GW + bit * GW, 1)
            )
            x = jnp.where((sy & bit) != 0, turned, x)
        wg[z, :, p * S:(p + 1) * S] = x.astype(jnp.bfloat16)
    lg[slot(b)] = lat[...]
    rp[b] = jnp.zeros((rows, depth), jnp.bfloat16)
    pl.semaphore_wait(barrier, (nz - 1) + (nb - 1) + (nv - 1))

    def w_copy(i):
        return send(wg.at[z], wg.at[z], w_s.at[i], w_r.at[z], along_z(i))

    def l_copy(i):
        return send(lat, lg.at[slot(b)], l_s.at[i], l_r.at[b], along_b(i))

    each(nb, lambda i: l_copy(i).start())
    each(nz, lambda i: w_copy(i).start())

    def w_wait(i):
        zt = lax.rem(z + i, nz)
        send(wg.at[zt], wg.at[zt], w_s.at[i], w_r.at[zt], along_z(i)).wait_recv()

    def l_wait(i):
        bt = lax.rem(b + i, nb)
        send(lat, lg.at[slot(bt)], l_s.at[i], l_r.at[bt], along_b(i)).wait_recv()

    each(nz, w_wait)
    panel = wg[...].reshape(wide, depth)
    f32 = panel.astype(jnp.float32)
    square = jnp.sum(f32 * f32, axis=1, keepdims=True)
    diagonal = lax.broadcasted_iota(jnp.int32, (wide, wide), 0) == lax.broadcasted_iota(
        jnp.int32, (wide, wide), 1
    )
    square = jnp.sum(jnp.where(diagonal, square, 0.0), axis=0, keepdims=True)
    each(nb, l_wait)
    gram = lax.dot_general(
        lg[...].reshape(nb * rows, depth), panel, (((1,), (1,)), ((), ())), preferred_element_type=jnp.float32
    )
    part[...] = (square - 2.0 * gram).reshape(nb, rows, wide)

    def r_copy(i):
        vt = lax.rem(v + i, nv)
        return send(part.at[slot(vt)], rv.at[v], r_s.at[i], r_r.at[v], along_v(i))

    each(nv, lambda i: r_copy(i).start())
    rv[v] = part[slot(v)]

    def r_wait(i):
        vt = lax.rem(v + i, nv)
        send(part.at[slot(vt)], rv.at[vt], r_s.at[i], r_r.at[vt], along_v(i)).wait_recv()

    each(nv, r_wait)
    volume = float(nv * depth)
    entropy = 0.5 / math.sqrt(volume)
    mine = pl.ds(pl.multiple_of(b * wide, wide), wide)
    g[k, l, :, mine] = jnp.sum(rv[...], axis=0) * (LOG2E / (volume * entropy))

    n_plane = nl * nb
    own = l * nb + b

    def g_copy(i):
        q = lax.rem(own + i, n_plane)
        here = g.at[k, l, :, mine]
        return send(here, here, g_s.at[i], g_r.at[own], at(z, lax.rem(q, nb), (q // nb) * 2 + k))

    each(n_plane, lambda i: g_copy(i).start())

    def g_wait(i):
        q = lax.rem(own + i, n_plane)
        bt, lt = lax.rem(q, nb), q // nb
        here = g.at[k, lt, :, pl.ds(pl.multiple_of(bt * wide, wide), wide)]
        send(here, here, g_s.at[i], g_r.at[q], at(z, bt, lt * 2 + k)).wait_recv()

    each(n_plane, g_wait)
    other = at(z, b, l * 2 + (1 - k))
    send(g.at[k], g.at[k], h_s, h_r, other).start()
    send(g.at[1 - k], g.at[1 - k], h_s, h_r, other).wait_recv()

    n = nz * nb * rows
    height = nb * rows
    urow[...] = jnp.zeros((1, n), jnp.float32)
    for it in range(ITERS):
        cost = g[...].reshape(height, n)
        t = urow[...] - cost
        top = jnp.max(t, axis=1, keepdims=True)
        total = jnp.sum(jnp.exp2(t - top), axis=1, keepdims=True)
        t = -(top + jnp.log2(total)) - cost
        top = jnp.max(t, axis=0, keepdims=True)
        total = jnp.sum(jnp.exp2(t - top), axis=0, keepdims=True)
        ex[it, z] = top + jnp.log2(total)

        def e_copy(i):
            here = ex.at[it, z]
            return send(here, here, e_s.at[it, i], e_r.at[it, z], along_z(i))

        def e_wait(i):
            zt = lax.rem(z + i, nz)
            here = ex.at[it, zt]
            send(here, here, e_s.at[it, i], e_r.at[it, zt], along_z(i)).wait_recv()

        each(nz, lambda i: e_copy(i).start())
        each(nz, e_wait)
        parts = ex[it]
        top = jnp.max(parts, axis=0)
        total = jnp.sum(jnp.exp2(parts - top[None]), axis=0)
        urow[...] = -(top + jnp.log2(total))

    t = urow[...] - g[...].reshape(height, n)
    top = jnp.max(t, axis=1, keepdims=True)
    total = jnp.sum(jnp.exp2(t - top), axis=1, keepdims=True)
    t = urow[:, mine] - g[:, :, :, mine].reshape(height, wide)
    weights = (jnp.exp2(t - top) / total).astype(jnp.bfloat16)

    coupled = jnp.dot(weights, wg[...].reshape(wide, depth), preferred_element_type=jnp.float32)
    pf[...] = coupled.reshape(nb, rows, depth)
    pb[...] = coupled.astype(jnp.bfloat16).reshape(nb, rows, depth)

    def c_copy(i):
        bt = lax.rem(b + i, nb)
        return send(pb.at[slot(bt)], rp.at[b], c_s.at[i], c_r.at[b], along_b(i))

    def c_wait(i):
        bt = lax.rem(b + i, nb)
        send(pb.at[slot(bt)], rp.at[bt], c_s.at[i], c_r.at[bt], along_b(i)).wait_recv()

    each(nb, lambda i: c_copy(i).start())
    each(nb, c_wait)
    total = pf[slot(b)]
    for j in range(nb):
        total = total + rp[j].astype(jnp.float32)
    tiles = []
    for p in range(patches):
        cut = slice(p * S, (p + 1) * S)
        tiles.append((1.0 - tv) * lat[:, cut].astype(jnp.float32) + tv * total[:, cut])
    mixed = jnp.concatenate(tiles, axis=0)
    mt[...] = mixed.T.astype(jnp.bfloat16).reshape(nv, st, patches * rows)

    def a_copy(i):
        vt = lax.rem(v + i, nv)
        return send(mt.at[vt], ra.at[v], a_s.at[i], a_r.at[v], along_v(i))

    def a_wait(i):
        vt = lax.rem(v + i, nv)
        send(mt.at[vt], ra.at[vt], a_s.at[i], a_r.at[vt], along_v(i)).wait_recv()

    each(nv, lambda i: a_copy(i).start())
    ra[v] = mt[v]
    each(nv, a_wait)
    out[...] = ra[...]

    each(nz, lambda i: w_copy(i).wait_send())
    each(nb, lambda i: l_copy(i).wait_send())
    each(nv, lambda i: r_copy(i).wait_send())
    each(n_plane, lambda i: g_copy(i).wait_send())
    send(g.at[k], g.at[k], h_s, h_r, other).wait_send()
    for it in range(ITERS):
        each(nz, lambda i: send(ex.at[it, z], ex.at[it, z], e_s.at[it, i], e_r.at[it, z], along_z(i)).wait_send())
    each(nb, lambda i: c_copy(i).wait_send())
    each(nv, lambda i: a_copy(i).wait_send())


def embed_tokens(tokens, table, out, x):
    nv, st, width = tokens.shape
    rows = out.shape[0]
    patches = width // rows

    @pl.when(pl.program_id(0) == 0)
    def _():
        clip_of = lax.broadcasted_iota(jnp.int32, (rows, st, width), 0)
        lane = lax.broadcasted_iota(jnp.int32, (rows, st, width), 2)
        keep = (lane & (rows - 1)) == clip_of
        from_lane = lax.broadcasted_iota(jnp.int32, (width, nv * patches), 0) // rows
        to_patch = lax.broadcasted_iota(jnp.int32, (width, nv * patches), 1)
        total = jnp.zeros((rows * st, nv * patches), jnp.float32)
        for j in range(nv):
            spread = jnp.where(keep, tokens[j].astype(jnp.float32)[None], 0.0)
            spread = spread.reshape(rows * st, width).astype(jnp.bfloat16)
            pick = jnp.where(to_patch == from_lane + j * patches, 1.0, 0.0).astype(jnp.bfloat16)
            total = total + jnp.dot(spread, pick, preferred_element_type=jnp.float32)
        x[...] = total.astype(jnp.bfloat16)

    made = jnp.dot(x[...], table[...], preferred_element_type=jnp.float32)
    out[...] = made.astype(jnp.bfloat16).reshape(out.shape)


def on_device(nc, nv, latents, noise, offsets, times, embed):
    nb = nv
    nz = nc // nb
    nl = nv // 2
    rows, depth = latents.shape
    patches = depth // S
    st = S // nv
    wide = nz * rows
    n = nc * rows
    f32, bf16 = jnp.float32, jnp.bfloat16
    dma = pltpu.SemaphoreType.DMA
    vmem = pl.BlockSpec(memory_space=pltpu.VMEM)
    smem = pl.BlockSpec(memory_space=pltpu.SMEM)
    sems = []
    for count in ((nz,), (nb,), (nv,), (nl * nb,), (), (ITERS, nz), (nb,), (nv,)):
        sems += [dma(count), dma(count)]
    tokens = pl.pallas_call(
        functools.partial(couple, nz, nb, nv),
        out_shape=jax.ShapeDtypeStruct((nv, st, patches * rows), bf16),
        in_specs=[vmem, vmem, smem, smem],
        out_specs=vmem,
        scratch_shapes=[
            pltpu.VMEM((nz, rows, depth), bf16),
            pltpu.VMEM((nb, rows, depth), bf16),
            pltpu.VMEM((nb, rows, wide), f32),
            pltpu.VMEM((nv, rows, wide), f32),
            pltpu.VMEM((2, nl, rows, n), f32),
            pltpu.VMEM((ITERS, nz, 1, n), f32),
            pltpu.VMEM((1, n), f32),
            pltpu.VMEM((nb, rows, depth), f32),
            pltpu.VMEM((nb, rows, depth), bf16),
            pltpu.VMEM((nb, rows, depth), bf16),
            pltpu.VMEM((nv, st, patches * rows), bf16),
            pltpu.VMEM((nv, st, patches * rows), bf16),
            *sems,
        ],
        compiler_params=pltpu.CompilerParams(collective_id=0, has_side_effects=True),
        name="couple",
    )(latents, noise, offsets.reshape(rows, 4), times)
    width = embed.shape[1]
    tile = min(width, 1024)
    return pl.pallas_call(
        embed_tokens,
        grid=(width // tile,),
        out_shape=jax.ShapeDtypeStruct((rows, st, width), bf16),
        in_specs=[
            pl.BlockSpec(tokens.shape, lambda i: (0, 0, 0)),
            pl.BlockSpec((embed.shape[0], tile), lambda i: (0, i)),
        ],
        out_specs=pl.BlockSpec((rows, st, tile), lambda i: (0, 0, i)),
        scratch_shapes=[pltpu.VMEM((rows * st, embed.shape[0]), bf16)],
        name="embed",
    )(tokens, embed)


def solution(mesh):
    placed = (P("clip", "val"), P("clip", "val"), P("clip", None, None), P("clip"), P())
    return jax.shard_map(
        functools.partial(on_device, mesh.shape["clip"], mesh.shape["val"]),
        mesh=mesh,
        in_specs=placed,
        out_specs=P("clip", "val", None),
        check_vma=False,
    )
```

time: 2140 us -> 82.7 us (0.04)
  blocking collectives: 1760 us -> 0 us
  waiting for transfers between devices: 191 us -> 0 us
  local copies, waits for them, and re-layouts: 148 us -> 1.35 us
  Pallas kernels: 0 us -> 81.1 us
    psum x5 -> x0, blocking collectives: 767 us -> none  [the longest x4 750 us: column_lse(): total = lax.psum(jnp.sum(jnp.exp(scores - top[None, :]), axis=0), 'clip')]
    pmax x4 -> x0, blocking collectives: 764 us -> none  [column_lse(): top = lax.pmax(top, 'clip')]
    all_to_all x1 -> x0, blocking collectives: 230 us -> none  [on_device(): lax.all_to_all(value_cube, 'val', split_axis=2, concat_axis=1, tiled=True)]
    gather x1 -> x0, local copies, waits for them, and re-layouts: 145 us -> none  [warp_noise(): return jnp.take_along_axis(value_cube, source, axis=2).reshape(noise.shape)]
    all_gather x1 -> x0, waiting for transfers between devices: 135 us -> none  [on_device(): panel_all = lax.all_gather(warped, 'clip', axis=0, tiled=True)]
    pallas_call x0 -> x2, Pallas kernels: none -> 81.1 us  [the longest x1 76.1 us: on_device(): pl.pallas_call(functools.partial(couple, nz, nb, nv), out_shape=jax.Shape...]
    psum x1 -> x0, waiting for transfers between devices: 55.7 us -> none  [on_device(): gram, square = lax.psum((gram_part, square_part), 'val')]
  transfers between devices with their start and end apart: 2 -> 0, of which waited for: 2 -> 0; matrix products, arithmetic and copies ran while one was open for 0% -> 0% of each run, Pallas kernels for 0% -> 0%
where the time goes in v1:
time: 82.7 us; the launch traced here: 82.5 us
  Pallas kernels  81.1 us (98%)
  local copies, waits for them, and re-layouts  1.35 us (2%)
    pallas_call x1, Pallas kernels, on_device(): pl.pallas_call(functools.partial(couple, nz, nb, nv), out_shape=jax.Shape...  76.1 us
    pallas_call x1, Pallas kernels, on_device(): pl.pallas_call(embed_tokens, grid=(width // tile,), out_shape=jax.ShapeDt...  4.97 us

profile of v1, /device:TPU:1, one launch (start us, length us, event | category | flops | bytes accessed | tf_op | source)
XLA Modules:
  0.0 82.5 jit_solution(28847789349247720)
XLA Ops:
  0.0 1.4 %copy.6.off = s32[16,4]{1,0:T(8,128)} copy(s32[16,4]{0,1:T(4,128)} %bitcast.1) | data formatting | bytes 512 | tf_op jit(solution)/shard_map/reshape | solution.py:305
  1.4 76.1 %couple.1.tokens = bf16[8,16,128]{2,1,0:T(8,128)(2,1)} custom-call(bf16[16,1024]{1,0:T(8,128)(2,1)} %lat.1, bf16[16,1024]{1,0:T(8,128)(2,1)} %noise.1, s32[16,4]{1,0:T(8,128)} %copy.6.off, f32[16]{0:T(128)} %times.1), custom_call_target="tpu_custom_call" | custom-call | tf_op jit(solution)/shard_map/couple/pallas_call | solution.py:283
  77.5 5.0 %embed.1 = bf16[16,16,5120]{2,1,0:T(8,128)(2,1)} custom-call(bf16[8,16,128]{2,1,0:T(8,128)(2,1)} %couple.1.tokens, bf16[64,5120]{1,0:T(8,128)(2,1)} %table.1), custom_call_target="tpu_custom_call" | custom-call | tf_op jit(solution)/shard_map/embed/pallas_call | solution.py:308

commit v2 on v0

v2 whole, which is shorter than its diff:
```python
import functools
import math

import jax
import jax.numpy as jnp
from jax import lax
from jax.experimental import pallas as pl
from jax.experimental.pallas import tpu as pltpu
from jax.sharding import PartitionSpec as P

P_SIZE = 64
FR = 2
GW = 16
GH = 4
ITERS = 4
STOP = 99
S = FR * GH * GW
LOG2E = 1.4426950408889634


def each(n, step):
    def body(i, carry):
        step(i)
        return carry

    lax.fori_loop(0, n, body, 0)


def far_first(n, i):
    return n // 2 + (2 * lax.rem(i, 2) - 1) * ((i + 1) // 2)


def turn(x, patches):
    return jnp.concatenate([x[:, p * S:(p + 1) * S] for p in range(patches)], axis=0).T


def couple(nz, nb, nv, lat, noise, off, times, out, pw, lg, part, rv, g, ex, urow, pb, rp, ms, la,
           w_s, w_r, l_s, l_r, r_s, r_r, g_s, g_r, e_s, e_r, c_s, c_r, a_s, a_r, p_s, p_r):
    nl, nx = nv // 2, nb // 2
    rows, depth = lat.shape
    patches = depth // S
    wide = nz * rows
    n = nb * wide
    st = S // nv
    width = patches * rows
    clip = lax.axis_index("clip")
    v = lax.axis_index("val")
    z, b = clip // nb, lax.rem(clip, nb)
    h, x = b // nx, lax.rem(b, nx)
    l, k = v // 2, lax.rem(v, 2)
    left = []

    def at(z_, b_, v_):
        return {"clip": z_ * nb + b_, "val": v_}

    def send(src, dst, s_sem, r_sem, where):
        return pltpu.make_async_remote_copy(src, dst, s_sem, r_sem, device_id=where)

    def launch(count, copy):
        each(count, lambda i: copy(i).start())
        left.append(lambda: each(count, lambda i: copy(i).wait_send()))

    def finish():
        for step in left:
            step()

    def halt(stage, value):
        if STOP != stage:
            return False
        out[...] = jnp.broadcast_to(jnp.sum(value), out.shape).astype(out.dtype)
        finish()
        return True

    def z_of(i):
        return lax.rem(z + far_first(nz, i), nz)

    def b_of(i):
        return jnp.where(i < nx, (1 - h) * nx + lax.rem(x + i, nx), h * nx + lax.rem(x + i + 1, nx))

    def v_of(i):
        return lax.rem(v + 1 + i, nv)

    barrier = pltpu.get_barrier_semaphore()
    each(nb - 1, lambda i: pl.semaphore_signal(barrier, inc=1, device_id=at(z, b_of(i), v)))
    each(nz - 1, lambda i: pl.semaphore_signal(barrier, inc=1, device_id=at(z_of(i), b, v)))
    each(nv - 1, lambda i: pl.semaphore_signal(barrier, inc=1, device_id=at(z, b, v_of(i))))

    rowi = lax.broadcasted_iota(jnp.int32, (rows, S), 0)
    lane = lax.broadcasted_iota(jnp.int32, (rows, S), 1)
    first = lane < GH * GW
    sy = jnp.zeros((rows, S), jnp.int32)
    sx = jnp.zeros((rows, S), jnp.int32)
    for i in range(rows):
        here = rowi == i
        sy = jnp.where(here, jnp.where(first, off[0, i], off[2, i]), sy)
        sx = jnp.where(here, jnp.where(first, off[1, i], off[3, i]), sx)
    col = lane & (GW - 1)
    row = (lane // GW) & (GH - 1)
    for p in range(patches):
        t = noise[:, p * S:(p + 1) * S].astype(jnp.float32)
        for bit in (1, 2, 4, 8):
            turned = jnp.where(col >= bit, pltpu.roll(t, bit, 1), pltpu.roll(t, S - GW + bit, 1))
            t = jnp.where((sx & bit) != 0, turned, t)
        for bit in (1, 2):
            turned = jnp.where(
                row >= bit, pltpu.roll(t, bit * GW, 1), pltpu.roll(t, S - GH * GW + bit * GW, 1)
            )
            t = jnp.where((sy & bit) != 0, turned, t)
        pw[h, k, z, :, p * S:(p + 1) * S] = t.astype(jnp.bfloat16)
    lg[b] = lat[...]
    pl.semaphore_wait(barrier, (nz - 1) + (nb - 1) + (nv - 1))
    if halt(0, sx.astype(jnp.float32)):
        return

    launch(nb - 1, lambda i: send(lat, lg.at[b], l_s.at[i], l_r.at[b], at(z, b_of(i), v)))
    mine = pw.at[h, k, z]
    launch(nz - 1, lambda i: send(mine, mine, w_s.at[i], w_r.at[z], at(z_of(i), b, v)))

    ms[...] = turn(lat[...].astype(jnp.float32), patches).astype(jnp.bfloat16).reshape(nv, st, width)
    launch(nv - 1, lambda i: send(ms.at[v_of(i)], la.at[v], a_s.at[i], a_r.at[v], at(z, b, v_of(i))))
    la[v] = ms[v]

    def w_wait(i):
        here = pw.at[h, k, z_of(i)]
        send(here, here, w_s.at[i], w_r.at[z_of(i)], at(z_of(i), b, v)).wait_recv()

    def l_wait(i):
        bt = b_of(i)
        send(lat, lg.at[bt], l_s.at[i], l_r.at[bt], at(z, bt, v)).wait_recv()

    each(nz - 1, w_wait)
    neighbour = at(z, b, l * 2 + (1 - k))
    facing = at(z, (1 - h) * nx + x, v)
    panel = pw.at[h, k]
    launch(1, lambda i: send(panel, panel, p_s.at[0], p_r.at[0], neighbour))
    noises = pw[h, k].reshape(wide, depth)
    square = noises.astype(jnp.float32)
    square = jnp.sum(square * square, axis=1, keepdims=True)
    diagonal = lax.broadcasted_iota(jnp.int32, (wide, wide), 0) == lax.broadcasted_iota(
        jnp.int32, (wide, wide), 1
    )
    square = jnp.sum(jnp.where(diagonal, square, 0.0), axis=0, keepdims=True)

    def block(half):
        gram = lax.dot_general(
            lg[pl.ds(half * nx, nx)].reshape(nx * rows, depth),
            pw[h, k].reshape(wide, depth),
            (((1,), (1,)), ((), ())),
            preferred_element_type=jnp.float32,
        )
        part[pl.ds(half * nx, nx)] = (square - 2.0 * gram).reshape(nx, rows, wide)

    def r_copy(vt):
        return send(part.at[vt], rv.at[v], r_s.at[vt], r_r.at[v], at(z, b, vt))

    def r_send(half):
        def one(i):
            vt = half * nx + lax.rem(x + i, nx)

            @pl.when(vt != v)
            def _():
                r_copy(vt).start()

        each(nx, one)

    each(nx - 1, lambda i: l_wait(nx + i))
    block(h)
    r_send(h)
    each(nx, l_wait)
    block(1 - h)
    r_send(1 - h)
    left.append(lambda: each(nv - 1, lambda i: r_copy(v_of(i)).wait_send()))
    rv[v] = part[v]
    if halt(1, part[0]):
        return

    def r_wait(i):
        vt = v_of(i)
        send(part.at[vt], rv.at[vt], r_s.at[vt], r_r.at[vt], at(z, b, vt)).wait_recv()

    each(nv - 1, r_wait)
    volume = float(nv * depth)
    entropy = 0.5 / math.sqrt(volume)

    def columns(b_):
        return pl.ds(pl.multiple_of(b_ * wide, wide), wide)

    g[l, :, columns(b)] = jnp.sum(rv[...], axis=0) * (LOG2E / (volume * entropy))
    if halt(2, g[l, :, columns(b)]):
        return

    n_plane = nl * nb
    own = l * nb + b

    def g_of(i):
        return lax.rem(own + 1 + i, n_plane)

    def g_at(q):
        return at(z, lax.rem(q, nb), (q // nb) * 2 + k)

    source = g.at[l, :, columns(b)]
    launch(n_plane - 1, lambda i: send(source, source, g_s.at[i], g_r.at[own], g_at(g_of(i))))

    def g_wait(i):
        q = g_of(i)
        here = g.at[q // nb, :, columns(lax.rem(q, nb))]
        send(here, here, g_s.at[i], g_r.at[q], g_at(q)).wait_recv()

    each(n_plane - 1, g_wait)
    launch(1, lambda i: send(panel, panel, p_s.at[1], p_r.at[1], facing))
    if halt(3, g[...]):
        return

    blocks = n // S
    height = nl * rows
    n_ring = 2 * nz
    own_e = z * 2 + k

    def tile(c, first=0, count=nl):
        return g[pl.ds(first, count), :, c * S:(c + 1) * S].reshape(count * rows, S)

    def row_stats(dual, first=0, count=nl):
        top = dual[0:1] - tile(0, first, count)
        for c in range(1, blocks):
            top = jnp.maximum(top, dual[c:c + 1] - tile(c, first, count))
        top = jnp.max(top, axis=1, keepdims=True)
        total = jnp.exp2(dual[0:1] - tile(0, first, count) - top)
        for c in range(1, blocks):
            total = total + jnp.exp2(dual[c:c + 1] - tile(c, first, count) - top)
        return top, jnp.sum(total, axis=1, keepdims=True)

    def e_of(i):
        return lax.rem(own_e + far_first(n_ring, i), n_ring)

    def e_at(q):
        return at(q // 2, b, l * 2 + lax.rem(q, 2))

    dual = jnp.zeros((blocks, S), jnp.float32)
    for it in range(ITERS):
        top, total = row_stats(dual)
        row_dual = -(top + jnp.log2(total))
        for c in range(blocks):
            t = row_dual - tile(c)
            top = jnp.max(t, axis=0, keepdims=True)
            total = jnp.sum(jnp.exp2(t - top), axis=0, keepdims=True)
            ex[it, own_e, c:c + 1] = top + jnp.log2(total)
        here = ex.at[it, own_e]

        def e_copy(i, it=it, here=here):
            return send(here, here, e_s.at[it, i], e_r.at[it, own_e], e_at(e_of(i)))

        def e_wait(i, it=it):
            q = e_of(i)
            there = ex.at[it, q]
            send(there, there, e_s.at[it, i], e_r.at[it, q], e_at(q)).wait_recv()

        launch(n_ring - 1, e_copy)
        if it == ITERS - 1:
            passed = pw.at[1 - h, k]
            send(passed, passed, p_s.at[1], p_r.at[1], facing).wait_recv()
            launch(1, lambda i: send(passed, passed, p_s.at[2], p_r.at[2], neighbour))
        each(n_ring - 1, e_wait)
        parts = ex[it]
        top = jnp.max(parts, axis=0)
        total = jnp.sum(jnp.exp2(parts - top[None]), axis=0)
        dual = -(top + jnp.log2(total))
        if halt(4 + it, dual):
            return

    for c in range(blocks):
        urow[:, c * S:(c + 1) * S] = dual[c:c + 1]
    count = nl // 2
    start = h * count
    top, total = row_stats(dual, start, count)
    weights = []
    for half in range(2):
        here = columns(half * nx + x)
        t = urow[:, here] - g[pl.ds(start, count), :, here].reshape(count * rows, wide)
        weights.append((jnp.exp2(t - top) / total).astype(jnp.bfloat16))

    there = pw.at[h, 1 - k]
    send(there, there, p_s.at[0], p_r.at[0], neighbour).wait_recv()
    there = pw.at[1 - h, 1 - k]
    send(there, there, p_s.at[2], p_r.at[2], neighbour).wait_recv()
    for kk in range(2):
        coupled = jnp.dot(weights[0], pw[0, kk].reshape(wide, depth), preferred_element_type=jnp.float32)
        coupled += jnp.dot(weights[1], pw[1, kk].reshape(wide, depth), preferred_element_type=jnp.float32)
        for i in range(count):
            piece = turn(coupled[i * rows:(i + 1) * rows], patches).astype(jnp.bfloat16)
            pb[i, :, kk] = piece.reshape(nv, st, width)
    if halt(8, pb[0, 0, 0].astype(jnp.float32)):
        return

    def c_copy(i, vt):
        return send(pb.at[i, vt], rp.at[x, l], c_s.at[i * nv + vt], c_r.at[x * nl + l], at(z, h * nx + 2 * i + k, vt))

    def c_each(act):
        def one(j):
            i, vt = j // nv, lax.rem(v + j, nv)

            @pl.when((2 * i + k != x) | (vt != v))
            def _():
                act(i, vt)

        each(count * nv, one)

    c_each(lambda i, vt: c_copy(i, vt).start())
    left.append(lambda: c_each(lambda i, vt: c_copy(i, vt).wait_send()))
    parity = lax.rem(x, 2)

    @pl.when(parity == k)
    def _():
        rp[x, l] = pb[x // 2, v]

    def c_wait(q):
        xt, lt = q // nl, lax.rem(q, nl)
        vt = lt * 2 + parity

        @pl.when((xt != x) | (vt != v))
        def _():
            send(pb.at[0, 0], rp.at[xt, lt], c_s.at[0], c_r.at[q], at(z, h * nx + xt, vt)).wait_recv()

    def a_wait(i):
        vt = v_of(i)
        send(ms.at[vt], la.at[vt], a_s.at[i], a_r.at[vt], at(z, b, vt)).wait_recv()

    lane = lax.broadcasted_iota(jnp.int32, (st, width), 1) & (rows - 1)
    time = jnp.zeros((st, width), jnp.float32)
    for i in range(rows):
        time = jnp.where(lane == i, times[i], time)
    clip_of = lax.broadcasted_iota(jnp.int32, (rows, st, width), 0)
    keep = (lax.broadcasted_iota(jnp.int32, (rows, st, width), 2) & (rows - 1)) == clip_of
    from_lane = lax.broadcasted_iota(jnp.int32, (width, nv * patches), 0) // rows
    to_patch = lax.broadcasted_iota(jnp.int32, (width, nv * patches), 1)
    each(nv - 1, a_wait)
    each(nx * nl, c_wait)
    made = jnp.zeros((rows * st, nv * patches), jnp.float32)
    for j in range(nv):
        coupled = rp[0, j // 2, j % 2].astype(jnp.float32)
        for xt in range(1, nx):
            coupled = coupled + rp[xt, j // 2, j % 2].astype(jnp.float32)
        mixed = (1.0 - time) * la[j].astype(jnp.float32) + time * coupled
        spread = jnp.where(keep, mixed[None], 0.0).reshape(rows * st, width).astype(jnp.bfloat16)
        pick = jnp.where(to_patch == from_lane + j * patches, 1.0, 0.0).astype(jnp.bfloat16)
        made = made + jnp.dot(spread, pick, preferred_element_type=jnp.float32)
    out[...] = made.astype(jnp.bfloat16)

    finish()


def on_device(nc, nv, latents, noise, offsets, times, embed):
    nb = nv
    nz, nl, nx = nc // nb, nv // 2, nb // 2
    rows, depth = latents.shape
    patches = depth // S
    st = S // nv
    wide = nz * rows
    n = nc * rows
    width = patches * rows
    f32, bf16 = jnp.float32, jnp.bfloat16
    dma = pltpu.SemaphoreType.DMA
    vmem = pl.BlockSpec(memory_space=pltpu.VMEM)
    smem = pl.BlockSpec(memory_space=pltpu.SMEM)
    sems = []
    for sent, got in (
        (nz, nz), (nb, nb), (nv, nv), (nl * nb, nl * nb), ((ITERS, 2 * nz),) * 2, (nl // 2 * nv, nx * nl), (nv, nv), (3, 3)
    ):
        sems += [dma(c if isinstance(c, tuple) else (c,)) for c in (sent, got)]
    tokens = pl.pallas_call(
        functools.partial(couple, nz, nb, nv),
        out_shape=jax.ShapeDtypeStruct((rows * st, nv * patches), bf16),
        in_specs=[vmem, vmem, smem, smem],
        out_specs=vmem,
        scratch_shapes=[
            pltpu.VMEM((2, 2, nz, rows, depth), bf16),
            pltpu.VMEM((nb, rows, depth), bf16),
            pltpu.VMEM((nb, rows, wide), f32),
            pltpu.VMEM((nv, rows, wide), f32),
            pltpu.VMEM((nl, rows, n), f32),
            pltpu.VMEM((ITERS, 2 * nz, n // S, S), f32),
            pltpu.VMEM((1, n), f32),
            pltpu.VMEM((nl // 2, nv, 2, st, width), bf16),
            pltpu.VMEM((nx, nl, 2, st, width), bf16),
            pltpu.VMEM((nv, st, width), bf16),
            pltpu.VMEM((nv, st, width), bf16),
            *sems,
        ],
        compiler_params=pltpu.CompilerParams(collective_id=0, has_side_effects=True),
        name="couple",
    )(latents, noise, offsets.reshape(rows, 4).T, times)
    made = jnp.dot(tokens, embed, preferred_element_type=f32).astype(bf16)
    return made.reshape(rows, st, embed.shape[1])


def solution(mesh):
    placed = (P("clip", "val"), P("clip", "val"), P("clip", None, None), P("clip"), P())
    return jax.shard_map(
        functools.partial(on_device, mesh.shape["clip"], mesh.shape["val"]),
        mesh=mesh,
        in_specs=placed,
        out_specs=P("clip", "val", None),
        check_vma=False,
    )
```

time: 2140 us -> 74.4 us (0.03)
  blocking collectives: 1760 us -> 0 us
  waiting for transfers between devices: 191 us -> 0 us
  local copies, waits for them, and re-layouts: 148 us -> 0.01 us
  Pallas kernels: 0 us -> 71 us
    psum x5 -> x0, blocking collectives: 767 us -> none  [the longest x4 750 us: column_lse(): total = lax.psum(jnp.sum(jnp.exp(scores - top[None, :]), axis=0), 'clip')]
    pmax x4 -> x0, blocking collectives: 764 us -> none  [column_lse(): top = lax.pmax(top, 'clip')]
    all_to_all x1 -> x0, blocking collectives: 230 us -> none  [on_device(): lax.all_to_all(value_cube, 'val', split_axis=2, concat_axis=1, tiled=True)]
    gather x1 -> x0, local copies, waits for them, and re-layouts: 145 us -> none  [warp_noise(): return jnp.take_along_axis(value_cube, source, axis=2).reshape(noise.shape)]
    all_gather x1 -> x0, waiting for transfers between devices: 135 us -> none  [on_device(): panel_all = lax.all_gather(warped, 'clip', axis=0, tiled=True)]
    pallas_call x0 -> x1, Pallas kernels: none -> 71 us  [on_device(): pl.pallas_call(functools.partial(couple, nz, nb, nv), out_shape=jax.Shape...]
    psum x1 -> x0, waiting for transfers between devices: 55.7 us -> none  [on_device(): gram, square = lax.psum((gram_part, square_part), 'val')]
  transfers between devices with their start and end apart: 2 -> 0, of which waited for: 2 -> 0; matrix products, arithmetic and copies ran while one was open for 0% -> 0% of each run, Pallas kernels for 0% -> 0%
where the time goes in v2:
time: 74.4 us; the launch traced here: 74.2 us
  Pallas kernels  71 us (95%)
  matrix products  3.15 us (4%)
    pallas_call x1, Pallas kernels, on_device(): pl.pallas_call(functools.partial(couple, nz, nb, nv), out_shape=jax.Shape...  71 us
    dot_general x1, matrix products, on_device(): made = jnp.dot(tokens, embed, preferred_element_type=f32).astype(bf16)  3.15 us

profile of v2, /device:TPU:1, one launch (start us, length us, event | category | flops | bytes accessed | tf_op | source)
XLA Modules:
  0.0 74.2 jit_solution(2328263063319802360)
XLA Ops:
  0.0 0.0 copy-start
  0.0 71.0 %couple.1 = bf16[256,64]{1,0:T(8,128)(2,1)} custom-call(bf16[16,1024]{1,0:T(8,128)(2,1)} %lat.1, bf16[16,1024]{1,0:T(8,128)(2,1)} %noise.1, s32[4,16]{1,0:T(4,128)} %bitcast.6, f32[16]{0:T(128)} %times.1), custom_call_target="tpu_custom_call" | custom-call | tf_op jit(solution)/shard_map/couple/pallas_call | solution.py:369
  71.0 0.0 copy-done
  71.0 3.2 %convolution_convert_fusion = bf16[256,5120]{1,0:T(8,128)(2,1)} fusion(bf16[256,64]{1,0:T(8,128)(2,1)} %couple.1, bf16[64,5120]{1,0:T(8,128)(2,1)S(1)} %copy-done), kind=kOutput, calls=%fused_computation | convolution fusion | flops 169082880 | bytes 3309568 | tf_op jit(solution)/shard_map/dot_general | solution.py:391
Async XLA Ops:
  0.0 71.0 %copy-start = (bf16[64,5120]{1,0:T(8,128)(2,1)S(1)}, bf16[64,5120]{1,0:T(8,128)(2,1)}, u32[]{:S(2)}) copy-start(bf16[64,5120]{1,0:T(8,128)(2,1)} %param.9) | copy-start | bytes 1966084

commit v3 on v2

v3 whole, which is shorter than its diff:
```python
import functools
import math

import jax
import jax.numpy as jnp
from jax import lax
from jax.experimental import pallas as pl
from jax.experimental.pallas import tpu as pltpu
from jax.sharding import PartitionSpec as P

P_SIZE = 64
FR = 2
GW = 16
GH = 4
ITERS = 4
S = FR * GH * GW
LOG2E = 1.4426950408889634


def ring(n):
    return sorted(range(1, n), key=lambda i: -min(i, n - i))


def turn(x, patches):
    return jnp.concatenate([x[:, p * S:(p + 1) * S] for p in range(patches)], axis=0).T


def couple(nz, nb, nv, lat, noise, off, times, out, pw, lg, part, rv, g, ex, urow, pb, rp, ms, la,
           w_s, w_r, l_s, l_near, l_far, r_s, r_r, g_s, g_r, e_s, e_r, c_s, c_r, a_s, a_r, p_s, p_r):
    nl, nx = nv // 2, nb // 2
    rows, depth = lat.shape
    patches = depth // S
    wide = nz * rows
    n = nb * wide
    st = S // nv
    width = patches * rows
    clip = lax.axis_index("clip")
    v = lax.axis_index("val")
    z, b = clip // nb, lax.rem(clip, nb)
    h, x = b // nx, lax.rem(b, nx)
    l, k = v // 2, lax.rem(v, 2)
    y = h * nl + l
    left = []

    def at(z_, b_, v_):
        return {"clip": z_ * nb + b_, "val": v_}

    def send(src, dst, s_sem, r_sem, where):
        pltpu.make_async_remote_copy(src, dst, s_sem, r_sem, device_id=where).start()

    def came(like, sem):
        pltpu.make_async_remote_copy(like, like, sem, sem, device_id=at(z, b, v)).wait_recv()

    def gone(like, sem):
        left.append(lambda: pltpu.make_async_remote_copy(like, like, sem, sem, device_id=at(z, b, v)).wait_send())

    def finish():
        while left:
            left.pop()()

    z_peers = [lax.rem(z + i, nz) for i in ring(nz)]
    far_peers = [(1 - h) * nx + lax.rem(x + i, nx) for i in ring(nx) + [0]]
    near_peers = [h * nx + lax.rem(x + i, nx) for i in ring(nx)]
    v_peers = [lax.rem(v + i, nv) for i in range(1, nv)]

    barrier = pltpu.get_barrier_semaphore()
    for bt in far_peers + near_peers:
        pl.semaphore_signal(barrier, inc=1, device_id=at(z, bt, v))
    for zt in z_peers:
        pl.semaphore_signal(barrier, inc=1, device_id=at(zt, b, v))
    for vt in v_peers:
        pl.semaphore_signal(barrier, inc=1, device_id=at(z, b, vt))

    rowi = lax.broadcasted_iota(jnp.int32, (rows, S), 0)
    lane = lax.broadcasted_iota(jnp.int32, (rows, S), 1)
    first = lane < GH * GW
    sy = jnp.zeros((rows, S), jnp.int32)
    sx = jnp.zeros((rows, S), jnp.int32)
    for i in range(rows):
        here = rowi == i
        sy = jnp.where(here, jnp.where(first, off[0, i], off[2, i]), sy)
        sx = jnp.where(here, jnp.where(first, off[1, i], off[3, i]), sx)
    col = lane & (GW - 1)
    row = (lane // GW) & (GH - 1)
    for p in range(patches):
        t = noise[:, p * S:(p + 1) * S].astype(jnp.float32)
        for bit in (1, 2, 4, 8):
            turned = jnp.where(col >= bit, pltpu.roll(t, bit, 1), pltpu.roll(t, S - GW + bit, 1))
            t = jnp.where((sx & bit) != 0, turned, t)
        for bit in (1, 2):
            turned = jnp.where(
                row >= bit, pltpu.roll(t, bit * GW, 1), pltpu.roll(t, S - GH * GW + bit * GW, 1)
            )
            t = jnp.where((sy & bit) != 0, turned, t)
        pw[h, k, z, :, p * S:(p + 1) * S] = t.astype(jnp.bfloat16)
    lg[b] = lat[...]
    pl.semaphore_wait(barrier, (nz - 1) + (nb - 1) + (nv - 1))

    for bt in far_peers:
        send(lat, lg.at[b], l_s, l_far, at(z, bt, v))
    for bt in near_peers:
        send(lat, lg.at[b], l_s, l_near, at(z, bt, v))
    gone(lg.at[pl.ds(0, nb - 1)], l_s)
    mine = pw.at[h, k, z]
    for zt in z_peers:
        send(mine, mine, w_s, w_r, at(zt, b, v))
    if nz > 1:
        gone(pw.at[h, k, pl.ds(0, nz - 1)], w_s)

    ms[...] = turn(lat[...].astype(jnp.float32), patches).astype(jnp.bfloat16).reshape(nv, st, width)
    for vt in v_peers:
        send(ms.at[vt], la.at[v], a_s, a_r, at(z, b, vt))
    gone(ms.at[pl.ds(0, nv - 1)], a_s)
    la[v] = ms[v]

    if nz > 1:
        came(pw.at[h, k, pl.ds(0, nz - 1)], w_r)
    neighbour = at(z, b, l * 2 + (1 - k))
    facing = at(z, (1 - h) * nx + x, v)
    panel = pw.at[h, k]
    send(panel, panel, p_s.at[0], p_r.at[0], neighbour)
    gone(panel, p_s.at[0])
    noises = pw[h, k].reshape(wide, depth)
    square = noises.astype(jnp.float32)
    square = jnp.sum(square * square, axis=1, keepdims=True)
    diagonal = lax.broadcasted_iota(jnp.int32, (wide, wide), 0) == lax.broadcasted_iota(
        jnp.int32, (wide, wide), 1
    )
    square = jnp.sum(jnp.where(diagonal, square, 0.0), axis=0, keepdims=True)

    def block(half):
        gram = lax.dot_general(
            lg[pl.ds(half * nx, nx)].reshape(nx * rows, depth),
            pw[h, k].reshape(wide, depth),
            (((1,), (1,)), ((), ())),
            preferred_element_type=jnp.float32,
        )
        part[pl.ds(half * nx, nx)] = (square - 2.0 * gram).reshape(nx, rows, wide)

    def r_send(half):
        for i in range(nx):
            vt = half * nx + lax.rem(x + i, nx)

            @pl.when(vt != v)
            def _():
                send(part.at[vt], rv.at[v], r_s, r_r, at(z, b, vt))

    came(lg.at[pl.ds(0, nx - 1)], l_near)
    block(h)
    r_send(h)
    came(lg.at[pl.ds(0, nx)], l_far)
    block(1 - h)
    r_send(1 - h)
    gone(part.at[pl.ds(0, nv - 1)], r_s)
    rv[v] = part[v]
    came(rv.at[pl.ds(0, nv - 1)], r_r)
    volume = float(nv * depth)
    entropy = 0.5 / math.sqrt(volume)

    piece = g.at[b * nl + l]
    piece[...] = jnp.sum(rv[...], axis=0) * (LOG2E / (volume * entropy))

    ny = 2 * nl
    steps = [(i, j) for i in range(ny) for j in range(nx) if i or j]
    for i, j in sorted(steps, key=lambda s: -min(s[0], ny - s[0]) - min(s[1], nx - s[1])):
        yt, xt = lax.rem(y + i, ny), lax.rem(x + j, nx)
        send(piece, piece, g_s, g_r, at(z, yt // nl * nx + xt, lax.rem(yt, nl) * 2 + k))
    pieces = g.at[pl.ds(0, nl * nb - 1)]
    gone(pieces, g_s)
    came(pieces, g_r)
    send(panel, panel, p_s.at[1], p_r.at[1], facing)
    gone(panel, p_s.at[1])

    blocks = nb
    own_e = z * 2 + k

    def tile(c, first=0, count=nl):
        return g[pl.ds(c * nl + first, count)].reshape(count * rows, wide)

    def row_stats(dual, first=0, count=nl):
        top = dual[0:1] - tile(0, first, count)
        for c in range(1, blocks):
            top = jnp.maximum(top, dual[c:c + 1] - tile(c, first, count))
        top = jnp.max(top, axis=1, keepdims=True)
        total = jnp.exp2(dual[0:1] - tile(0, first, count) - top)
        for c in range(1, blocks):
            total = total + jnp.exp2(dual[c:c + 1] - tile(c, first, count) - top)
        return top, jnp.sum(total, axis=1, keepdims=True)

    e_peers = [(z_, q) for z_ in z_peers for q in (1 - k, k)] + [(z, 1 - k)]

    dual = jnp.zeros((blocks, wide), jnp.float32)
    for it in range(ITERS):
        top, total = row_stats(dual)
        row_dual = -(top + jnp.log2(total))
        for c in range(blocks):
            t = row_dual - tile(c)
            top = jnp.max(t, axis=0, keepdims=True)
            total = jnp.sum(jnp.exp2(t - top), axis=0, keepdims=True)
            ex[it, own_e, c:c + 1] = top + jnp.log2(total)
        here = ex.at[it, own_e]

        for zt, kt in e_peers:
            send(here, here, e_s.at[it], e_r.at[it], at(zt, b, l * 2 + kt))
        others = ex.at[it, pl.ds(0, 2 * nz - 1)]
        gone(others, e_s.at[it])
        if it == ITERS - 1:
            passed = pw.at[1 - h, k]
            came(passed, p_r.at[1])
            send(passed, passed, p_s.at[2], p_r.at[2], neighbour)
            gone(passed, p_s.at[2])
        came(others, e_r.at[it])
        parts = ex[it]
        top = jnp.max(parts, axis=0)
        total = jnp.sum(jnp.exp2(parts - top[None]), axis=0)
        dual = -(top + jnp.log2(total))

    urow[...] = dual
    count = nl // 2
    start = h * count
    top, total = row_stats(dual, start, count)
    weights = []
    for half in range(2):
        at_x = half * nx + x
        t = urow[pl.ds(at_x, 1)] - g[pl.ds(at_x * nl + start, count)].reshape(count * rows, wide)
        weights.append((jnp.exp2(t - top) / total).astype(jnp.bfloat16))

    came(pw.at[h, 1 - k], p_r.at[0])
    came(pw.at[1 - h, 1 - k], p_r.at[2])
    for kk in range(2):
        coupled = jnp.dot(weights[0], pw[0, kk].reshape(wide, depth), preferred_element_type=jnp.float32)
        coupled += jnp.dot(weights[1], pw[1, kk].reshape(wide, depth), preferred_element_type=jnp.float32)
        for i in range(count):
            piece = turn(coupled[i * rows:(i + 1) * rows], patches).astype(jnp.bfloat16)
            pb[i * nv:(i + 1) * nv, kk] = piece.reshape(nv, st, width)

    parity = lax.rem(x, 2)
    slot = x * nl + l
    for vt in v_peers + [v]:
        for i in range(count):
            src, dst, xt = pb.at[i * nv + vt], rp.at[slot], 2 * i + k
            if vt is not v:
                send(src, dst, c_s, c_r, at(z, h * nx + xt, vt))
            else:

                @pl.when(xt != x)
                def _():
                    send(src, dst, c_s, c_r, at(z, h * nx + xt, vt))

    @pl.when(parity == k)
    def _():
        rp[slot] = pb[x // 2 * nv + v]

    finish()
    lane = lax.broadcasted_iota(jnp.int32, (st, width), 1) & (rows - 1)
    time = jnp.zeros((st, width), jnp.float32)
    for i in range(rows):
        time = jnp.where(lane == i, times[i], time)
    clip_of = lax.broadcasted_iota(jnp.int32, (rows, st, width), 0)
    keep = (lax.broadcasted_iota(jnp.int32, (rows, st, width), 2) & (rows - 1)) == clip_of
    from_lane = lax.broadcasted_iota(jnp.int32, (width, nv * patches), 0) // rows
    to_patch = lax.broadcasted_iota(jnp.int32, (width, nv * patches), 1)
    came(la.at[pl.ds(0, nv - 1)], a_r)
    number = nx * nl

    @pl.when(parity == k)
    def _():
        came(rp.at[pl.ds(0, number - 1)], c_r)

    @pl.when(parity != k)
    def _():
        came(rp, c_r)

    made = jnp.zeros((rows * st, nv * patches), jnp.float32)
    for j in range(nv):
        coupled = rp[j // 2, j % 2].astype(jnp.float32)
        for xt in range(1, nx):
            coupled = coupled + rp[xt * nl + j // 2, j % 2].astype(jnp.float32)
        mixed = (1.0 - time) * la[j].astype(jnp.float32) + time * coupled
        spread = jnp.where(keep, mixed[None], 0.0).reshape(rows * st, width).astype(jnp.bfloat16)
        pick = jnp.where(to_patch == from_lane + j * patches, 1.0, 0.0).astype(jnp.bfloat16)
        made = made + jnp.dot(spread, pick, preferred_element_type=jnp.float32)
    out[...] = made.astype(jnp.bfloat16)

    @pl.when(parity == k)
    def _():
        gone(pb.at[pl.ds(0, number - 1)], c_s)
        finish()

    @pl.when(parity != k)
    def _():
        gone(pb, c_s)
        finish()


def on_device(nc, nv, latents, noise, offsets, times, embed):
    nb = nv
    nz, nl, nx = nc // nb, nv // 2, nb // 2
    rows, depth = latents.shape
    patches = depth // S
    st = S // nv
    wide = nz * rows
    width = patches * rows
    f32, bf16 = jnp.float32, jnp.bfloat16
    vmem = pl.BlockSpec(memory_space=pltpu.VMEM)
    smem = pl.BlockSpec(memory_space=pltpu.SMEM)
    sems = []
    for shape in (1, 1, 1, 1, 1, 1, 1, 1, 1, ITERS, ITERS, 1, 1, 1, 1, 3, 3):
        sems.append(pltpu.SemaphoreType.DMA if shape == 1 else pltpu.SemaphoreType.DMA((shape,)))
    tokens = pl.pallas_call(
        functools.partial(couple, nz, nb, nv),
        out_shape=jax.ShapeDtypeStruct((rows * st, nv * patches), bf16),
        in_specs=[vmem, vmem, smem, smem],
        out_specs=vmem,
        scratch_shapes=[
            pltpu.VMEM((2, 2, nz, rows, depth), bf16),
            pltpu.VMEM((nb, rows, depth), bf16),
            pltpu.VMEM((nb, rows, wide), f32),
            pltpu.VMEM((nv, rows, wide), f32),
            pltpu.VMEM((nb * nl, rows, wide), f32),
            pltpu.VMEM((ITERS, 2 * nz, nb, wide), f32),
            pltpu.VMEM((nb, wide), f32),
            pltpu.VMEM((nl // 2 * nv, 2, st, width), bf16),
            pltpu.VMEM((nx * nl, 2, st, width), bf16),
            pltpu.VMEM((nv, st, width), bf16),
            pltpu.VMEM((nv, st, width), bf16),
            *sems,
        ],
        compiler_params=pltpu.CompilerParams(collective_id=0, has_side_effects=True),
        name="couple",
    )(latents, noise, offsets.reshape(rows, 4).T, times)
    made = jnp.dot(tokens, embed, preferred_element_type=f32).astype(bf16)
    return made.reshape(rows, st, embed.shape[1])


def solution(mesh):
    placed = (P("clip", "val"), P("clip", "val"), P("clip", None, None), P("clip"), P())
    return jax.shard_map(
        functools.partial(on_device, mesh.shape["clip"], mesh.shape["val"]),
        mesh=mesh,
        in_specs=placed,
        out_specs=P("clip", "val", None),
        check_vma=False,
    )
```

time: 74.4 us -> 69.9 us (0.940)
  Pallas kernels: 71 us -> 66.6 us
    pallas_call x1, Pallas kernels: 71 us -> 66.6 us  [on_device(): pl.pallas_call(functools.partial(couple, nz, nb, nv), out_shape=jax.Shape...]
where the time goes in v3:
time: 69.9 us; the launch traced here: 69.7 us
  Pallas kernels  66.6 us (95%)
  matrix products  3.15 us (5%)
    pallas_call x1, Pallas kernels, on_device(): pl.pallas_call(functools.partial(couple, nz, nb, nv), out_shape=jax.Shape...  66.6 us
    dot_general x1, matrix products, on_device(): made = jnp.dot(tokens, embed, preferred_element_type=f32).astype(bf16)  3.15 us

profile of v3, /device:TPU:1, one launch (start us, length us, event | category | flops | bytes accessed | tf_op | source)
XLA Modules:
  0.0 69.7 jit_solution(16019731575860263036)
XLA Ops:
  0.0 0.0 copy-start
  0.0 66.6 %couple.1 = bf16[256,64]{1,0:T(8,128)(2,1)} custom-call(bf16[16,1024]{1,0:T(8,128)(2,1)} %lat.1, bf16[16,1024]{1,0:T(8,128)(2,1)} %noise.1, s32[4,16]{1,0:T(4,128)} %bitcast.6, f32[16]{0:T(128)} %times.1), custom_call_target="tpu_custom_call" | custom-call | tf_op jit(solution)/shard_map/couple/pallas_call | solution.py:310
  66.6 0.0 copy-done
  66.6 3.2 %convolution_convert_fusion = bf16[256,5120]{1,0:T(8,128)(2,1)} fusion(bf16[256,64]{1,0:T(8,128)(2,1)} %couple.1, bf16[64,5120]{1,0:T(8,128)(2,1)S(1)} %copy-done), kind=kOutput, calls=%fused_computation | convolution fusion | flops 169082880 | bytes 3309568 | tf_op jit(solution)/shard_map/dot_general | solution.py:332
Async XLA Ops:
  0.0 66.6 %copy-start = (bf16[64,5120]{1,0:T(8,128)(2,1)S(1)}, bf16[64,5120]{1,0:T(8,128)(2,1)}, u32[]{:S(2)}) copy-start(bf16[64,5120]{1,0:T(8,128)(2,1)} %param.9) | copy-start | bytes 1966084

commit v4 on v3

--- a/solution.py
+++ b/solution.py
@@ -13,6 +13,7 @@
 GW = 16
 GH = 4
 ITERS = 4
+VMEM = 16 << 20
 S = FR * GH * GW
 LOG2E = 1.4426950408889634
 
@@ -25,8 +26,8 @@
     return jnp.concatenate([x[:, p * S:(p + 1) * S] for p in range(patches)], axis=0).T
 
 
-def couple(nz, nb, nv, lat, noise, off, times, out, pw, lg, part, rv, g, ex, urow, pb, rp, ms, la,
-           w_s, w_r, l_s, l_near, l_far, r_s, r_r, g_s, g_r, e_s, e_r, c_s, c_r, a_s, a_r, p_s, p_r):
+def couple(nz, nb, nv, lat_in, noise_in, off_in, times_in, out, lat, noise, off, times, pw, lg, part, rv, g, ex, urow, pb, rp, ms, la,
+           w_s, w_r, l_s, l_near, l_far, r_s, r_r, g_s, g_r, e_s, e_r, c_s, c_r, a_s, a_r, p_s, p_r, i_s):
     nl, nx = nv // 2, nb // 2
     rows, depth = lat.shape
     patches = depth // S
@@ -71,17 +72,26 @@
     for vt in v_peers:
         pl.semaphore_signal(barrier, inc=1, device_id=at(z, b, vt))
 
+    loads = [
+        pltpu.make_async_copy(src, dst, i_s.at[i])
+        for i, (src, dst) in enumerate(((off_in, off), (noise_in, noise), (lat_in, lat), (times_in, times)))
+    ]
+    for load in loads:
+        load.start()
+
     rowi = lax.broadcasted_iota(jnp.int32, (rows, S), 0)
     lane = lax.broadcasted_iota(jnp.int32, (rows, S), 1)
     first = lane < GH * GW
     sy = jnp.zeros((rows, S), jnp.int32)
     sx = jnp.zeros((rows, S), jnp.int32)
+    loads[0].wait()
     for i in range(rows):
         here = rowi == i
         sy = jnp.where(here, jnp.where(first, off[0, i], off[2, i]), sy)
         sx = jnp.where(here, jnp.where(first, off[1, i], off[3, i]), sx)
     col = lane & (GW - 1)
     row = (lane // GW) & (GH - 1)
+    loads[1].wait()
     for p in range(patches):
         t = noise[:, p * S:(p + 1) * S].astype(jnp.float32)
         for bit in (1, 2, 4, 8):
@@ -93,6 +103,8 @@
             )
             t = jnp.where((sy & bit) != 0, turned, t)
         pw[h, k, z, :, p * S:(p + 1) * S] = t.astype(jnp.bfloat16)
+    loads[2].wait()
+    loads[3].wait()
     lg[b] = lat[...]
     pl.semaphore_wait(barrier, (nz - 1) + (nb - 1) + (nv - 1))
 
@@ -303,16 +315,19 @@
     width = patches * rows
     f32, bf16 = jnp.float32, jnp.bfloat16
     vmem = pl.BlockSpec(memory_space=pltpu.VMEM)
-    smem = pl.BlockSpec(memory_space=pltpu.SMEM)
     sems = []
-    for shape in (1, 1, 1, 1, 1, 1, 1, 1, 1, ITERS, ITERS, 1, 1, 1, 1, 3, 3):
+    for shape in (1, 1, 1, 1, 1, 1, 1, 1, 1, ITERS, ITERS, 1, 1, 1, 1, 3, 3, 4):
         sems.append(pltpu.SemaphoreType.DMA if shape == 1 else pltpu.SemaphoreType.DMA((shape,)))
     tokens = pl.pallas_call(
         functools.partial(couple, nz, nb, nv),
         out_shape=jax.ShapeDtypeStruct((rows * st, nv * patches), bf16),
-        in_specs=[vmem, vmem, smem, smem],
+        in_specs=[pl.BlockSpec(memory_space=pltpu.HBM)] * 4,
         out_specs=vmem,
         scratch_shapes=[
+            pltpu.VMEM((rows, depth), bf16),
+            pltpu.VMEM((rows, depth), bf16),
+            pltpu.SMEM((4, rows), jnp.int32),
+            pltpu.SMEM((rows,), f32),
             pltpu.VMEM((2, 2, nz, rows, depth), bf16),
             pltpu.VMEM((nb, rows, depth), bf16),
             pltpu.VMEM((nb, rows, wide), f32),
@@ -326,9 +341,14 @@
             pltpu.VMEM((nv, st, width), bf16),
             *sems,
         ],
-        compiler_params=pltpu.CompilerParams(collective_id=0, has_side_effects=True),
+        compiler_params=pltpu.CompilerParams(
+            collective_id=0, has_side_effects=True, vmem_limit_bytes=VMEM
+        ),
         name="couple",
-    )(latents, noise, offsets.reshape(rows, 4).T, times)
+    )(*[
+        pltpu.with_memory_space_constraint(a, pltpu.HBM)
+        for a in (latents, noise, offsets.reshape(rows, 4).T, times)
+    ])
     made = jnp.dot(tokens, embed, preferred_element_type=f32).astype(bf16)
     return made.reshape(rows, st, embed.shape[1])
 

time: 69.9 us -> 67.7 us (0.969)
  Pallas kernels: 66.6 us -> 65.1 us
  matrix products: 3.15 us -> 2.32 us
    pallas_call x1, Pallas kernels: 66.6 us -> 65.1 us  [on_device(): pl.pallas_call(functools.partial(couple, nz, nb, nv), out_shape=jax.Shape...]
    dot_general x1, matrix products: 3.15 us -> 2.32 us  [on_device(): made = jnp.dot(tokens, embed, preferred_element_type=f32).astype(bf16)]
where the time goes in v4:
time: 67.7 us; the launch traced here: 67.5 us
  Pallas kernels  65.1 us (96%)
  matrix products  2.32 us (3%)
    pallas_call x1, Pallas kernels, on_device(): pl.pallas_call(functools.partial(couple, nz, nb, nv), out_shape=jax.Shape...  65.1 us
    dot_general x1, matrix products, on_device(): made = jnp.dot(tokens, embed, preferred_element_type=f32).astype(bf16)  2.32 us

profile of v4, /device:TPU:1, one launch (start us, length us, event | category | flops | bytes accessed | tf_op | source)
XLA Modules:
  0.0 67.5 jit_solution(10047408117827444347)
XLA Ops:
  0.0 0.0 copy-start
  0.0 65.1 %couple.1 = bf16[256,64]{1,0:T(8,128)(2,1)S(1)} custom-call(bf16[16,1024]{1,0:T(8,128)(2,1)} %lat_in.1, bf16[16,1024]{1,0:T(8,128)(2,1)} %noise_in.1, s32[4,16]{1,0:T(4,128)} %bitcast.6, f32[16]{0:T(128)} %times_in.1), custom_call_target="tpu_custom_call" | custom-call | tf_op jit(solution)/shard_map/couple/pallas_call | solution.py:321
  65.2 0.0 copy-done
  65.2 2.3 %convolution_convert_fusion = bf16[256,5120]{1,0:T(8,128)(2,1)} fusion(bf16[256,64]{1,0:T(8,128)(2,1)S(1)} %couple.1, bf16[64,5120]{1,0:T(8,128)(2,1)S(1)} %copy-done), kind=kOutput, calls=%fused_computation | convolution fusion | flops 169082880 | bytes 3309568 | tf_op jit(solution)/shard_map/dot_general | solution.py:352
Async XLA Ops:
  0.0 65.2 %copy-start = (bf16[64,5120]{1,0:T(8,128)(2,1)S(1)}, bf16[64,5120]{1,0:T(8,128)(2,1)}, u32[]{:S(2)}) copy-start(bf16[64,5120]{1,0:T(8,128)(2,1)} %param.9) | copy-start | bytes 1966084

commit v5 on v4

--- a/solution.py
+++ b/solution.py
@@ -27,7 +27,7 @@
 
 
 def couple(nz, nb, nv, lat_in, noise_in, off_in, times_in, out, lat, noise, off, times, pw, lg, part, rv, g, ex, urow, pb, rp, ms, la,
-           w_s, w_r, l_s, l_near, l_far, r_s, r_r, g_s, g_r, e_s, e_r, c_s, c_r, a_s, a_r, p_s, p_r, i_s):
+           w_s, w_r, l_s, l_near, l_far, r_s, r_r, g_s, g_r, e_s, e_r, c_s, c_r, a_s, a_r, p_s, p_r, i_s, f_s, f_r):
     nl, nx = nv // 2, nb // 2
     rows, depth = lat.shape
     patches = depth // S
@@ -173,13 +173,25 @@
     piece[...] = jnp.sum(rv[...], axis=0) * (LOG2E / (volume * entropy))
 
     ny = 2 * nl
-    steps = [(i, j) for i in range(ny) for j in range(nx) if i or j]
-    for i, j in sorted(steps, key=lambda s: -min(s[0], ny - s[0]) - min(s[1], nx - s[1])):
-        yt, xt = lax.rem(y + i, ny), lax.rem(x + j, nx)
-        send(piece, piece, g_s, g_r, at(z, yt // nl * nx + xt, lax.rem(yt, nl) * 2 + k))
-    pieces = g.at[pl.ds(0, nl * nb - 1)]
-    gone(pieces, g_s)
-    came(pieces, g_r)
+    x_peers = [lax.rem(x + i, nx) for i in ring(nx)]
+
+    def pass_on(h_, l_):
+        here = g.at[(h_ * nx + x) * nl + l_]
+        for xt in x_peers:
+            send(here, here, f_s, f_r, at(z, h * nx + xt, v))
+
+    for i in ring(ny):
+        yt = lax.rem(y + i, ny)
+        send(piece, piece, g_s, g_r.at[i], at(z, yt // nl * nx + x, lax.rem(yt, nl) * 2 + k))
+    pass_on(h, l)
+    for i in reversed(ring(ny)):
+        yt = lax.rem(y + ny - i, ny)
+        came(piece, g_r.at[i])
+        pass_on(yt // nl, lax.rem(yt, nl))
+    gone(g.at[pl.ds(0, ny - 1)], g_s)
+    pieces = g.at[pl.ds(0, ny * (nx - 1))]
+    gone(pieces, f_s)
+    came(pieces, f_r)
     send(panel, panel, p_s.at[1], p_r.at[1], facing)
     gone(panel, p_s.at[1])
 
@@ -239,25 +251,26 @@
 
     came(pw.at[h, 1 - k], p_r.at[0])
     came(pw.at[1 - h, 1 - k], p_r.at[2])
+    parity = lax.rem(x, 2)
+    slot = l * nx + x
+    partial = []
     for kk in range(2):
         coupled = jnp.dot(weights[0], pw[0, kk].reshape(wide, depth), preferred_element_type=jnp.float32)
-        coupled += jnp.dot(weights[1], pw[1, kk].reshape(wide, depth), preferred_element_type=jnp.float32)
-        for i in range(count):
-            piece = turn(coupled[i * rows:(i + 1) * rows], patches).astype(jnp.bfloat16)
-            pb[i * nv:(i + 1) * nv, kk] = piece.reshape(nv, st, width)
-
-    parity = lax.rem(x, 2)
-    slot = x * nl + l
-    for vt in v_peers + [v]:
-        for i in range(count):
-            src, dst, xt = pb.at[i * nv + vt], rp.at[slot], 2 * i + k
-            if vt is not v:
-                send(src, dst, c_s, c_r, at(z, h * nx + xt, vt))
-            else:
-
-                @pl.when(xt != x)
-                def _():
-                    send(src, dst, c_s, c_r, at(z, h * nx + xt, vt))
+        partial.append(
+            coupled + jnp.dot(weights[1], pw[1, kk].reshape(wide, depth), preferred_element_type=jnp.float32)
+        )
+
+    for i in range(count):
+        for kk in range(2):
+            made = turn(partial[kk][i * rows:(i + 1) * rows], patches).astype(jnp.bfloat16)
+            pb[i * nv:(i + 1) * nv, kk] = made.reshape(nv, st, width)
+        xt = 2 * i + k
+        for vt in v_peers:
+            send(pb.at[i * nv + vt], rp.at[slot], c_s, c_r.at[l], at(z, h * nx + xt, vt))
+
+        @pl.when(xt != x)
+        def _():
+            send(pb.at[i * nv + v], rp.at[slot], c_s, c_r.at[l], at(z, h * nx + xt, v))
 
     @pl.when(parity == k)
     def _():
@@ -274,24 +287,30 @@
     to_patch = lax.broadcasted_iota(jnp.int32, (width, nv * patches), 1)
     came(la.at[pl.ds(0, nv - 1)], a_r)
     number = nx * nl
-
-    @pl.when(parity == k)
-    def _():
-        came(rp.at[pl.ds(0, number - 1)], c_r)
-
-    @pl.when(parity != k)
-    def _():
-        came(rp, c_r)
-
     made = jnp.zeros((rows * st, nv * patches), jnp.float32)
-    for j in range(nv):
-        coupled = rp[j // 2, j % 2].astype(jnp.float32)
-        for xt in range(1, nx):
-            coupled = coupled + rp[xt * nl + j // 2, j % 2].astype(jnp.float32)
-        mixed = (1.0 - time) * la[j].astype(jnp.float32) + time * coupled
-        spread = jnp.where(keep, mixed[None], 0.0).reshape(rows * st, width).astype(jnp.bfloat16)
-        pick = jnp.where(to_patch == from_lane + j * patches, 1.0, 0.0).astype(jnp.bfloat16)
-        made = made + jnp.dot(spread, pick, preferred_element_type=jnp.float32)
+    for i in range(nl):
+        lt = lax.rem(l + i, nl)
+        if i == 0:
+
+            @pl.when(parity == k)
+            def _():
+                came(rp.at[pl.ds(0, nx - 1)], c_r.at[lt])
+
+            @pl.when(parity != k)
+            def _():
+                came(rp.at[pl.ds(0, nx)], c_r.at[lt])
+
+        else:
+            came(rp.at[pl.ds(0, nx)], c_r.at[lt])
+        for kk in range(2):
+            coupled = rp[lt * nx, kk].astype(jnp.float32)
+            for xt in range(1, nx):
+                coupled = coupled + rp[lt * nx + xt, kk].astype(jnp.float32)
+            mixed = (1.0 - time) * la[lt * 2 + kk].astype(jnp.float32) + time * coupled
+            spread = jnp.where(keep, mixed[None], 0.0).reshape(rows * st, width).astype(jnp.bfloat16)
+            start = (lt * 2 + kk) * patches
+            pick = jnp.where(to_patch == from_lane + start, 1.0, 0.0).astype(jnp.bfloat16)
+            made = made + jnp.dot(spread, pick, preferred_element_type=jnp.float32)
     out[...] = made.astype(jnp.bfloat16)
 
     @pl.when(parity == k)
@@ -316,7 +335,7 @@
     f32, bf16 = jnp.float32, jnp.bfloat16
     vmem = pl.BlockSpec(memory_space=pltpu.VMEM)
     sems = []
-    for shape in (1, 1, 1, 1, 1, 1, 1, 1, 1, ITERS, ITERS, 1, 1, 1, 1, 3, 3, 4):
+    for shape in (1, 1, 1, 1, 1, 1, 1, 1, 2 * nl, ITERS, ITERS, 1, nl, 1, 1, 3, 3, 4, 1, 1):
         sems.append(pltpu.SemaphoreType.DMA if shape == 1 else pltpu.SemaphoreType.DMA((shape,)))
     tokens = pl.pallas_call(
         functools.partial(couple, nz, nb, nv),

time: 67.7 us -> 66.6 us (0.984)
  Pallas kernels: 65.1 us -> 64 us
    pallas_call x1, Pallas kernels: 65.1 us -> 64 us  [on_device(): pl.pallas_call(functools.partial(couple, nz, nb, nv), out_shape=jax.Shape...]
where the time goes in v5:
time: 66.6 us; the launch traced here: 66.4 us
  Pallas kernels  64 us (96%)
  matrix products  2.32 us (3%)
    pallas_call x1, Pallas kernels, on_device(): pl.pallas_call(functools.partial(couple, nz, nb, nv), out_shape=jax.Shape...  64 us
    dot_general x1, matrix products, on_device(): made = jnp.dot(tokens, embed, preferred_element_type=f32).astype(bf16)  2.32 us

profile of v5, /device:TPU:1, one launch (start us, length us, event | category | flops | bytes accessed | tf_op | source)
XLA Modules:
  0.0 66.4 jit_solution(17015865853634641675)
XLA Ops:
  0.0 0.0 copy-start
  0.0 64.0 %couple.1 = bf16[256,64]{1,0:T(8,128)(2,1)S(1)} custom-call(bf16[16,1024]{1,0:T(8,128)(2,1)} %lat_in.1, bf16[16,1024]{1,0:T(8,128)(2,1)} %noise_in.1, s32[4,16]{1,0:T(4,128)} %bitcast.6, f32[16]{0:T(128)} %times_in.1), custom_call_target="tpu_custom_call" | custom-call | tf_op jit(solution)/shard_map/couple/pallas_call | solution.py:340
  64.1 0.0 copy-done
  64.1 2.3 %convolution_convert_fusion = bf16[256,5120]{1,0:T(8,128)(2,1)} fusion(bf16[256,64]{1,0:T(8,128)(2,1)S(1)} %couple.1, bf16[64,5120]{1,0:T(8,128)(2,1)S(1)} %copy-done), kind=kOutput, calls=%fused_computation | convolution fusion | flops 169082880 | bytes 3309568 | tf_op jit(solution)/shard_map/dot_general | solution.py:371
Async XLA Ops:
  0.0 64.1 %copy-start = (bf16[64,5120]{1,0:T(8,128)(2,1)S(1)}, bf16[64,5120]{1,0:T(8,128)(2,1)}, u32[]{:S(2)}) copy-start(bf16[64,5120]{1,0:T(8,128)(2,1)} %param.9) | copy-start | bytes 1966084

commit v6 on v5

--- a/solution.py
+++ b/solution.py
@@ -27,7 +27,7 @@
 
 
 def couple(nz, nb, nv, lat_in, noise_in, off_in, times_in, out, lat, noise, off, times, pw, lg, part, rv, g, ex, urow, pb, rp, ms, la,
-           w_s, w_r, l_s, l_near, l_far, r_s, r_r, g_s, g_r, e_s, e_r, c_s, c_r, a_s, a_r, p_s, p_r, i_s, f_s, f_r):
+           w_s, w_r, l_s, l_near, l_far, r_s, r_r, g_s, g_r, e_s, e_r, c_s, c_r, a_s, a_r, p_s, p_r, i_s, f_s, f_r, l_face, k_s):
     nl, nx = nv // 2, nb // 2
     rows, depth = lat.shape
     patches = depth // S
@@ -60,12 +60,13 @@
             left.pop()()
 
     z_peers = [lax.rem(z + i, nz) for i in ring(nz)]
-    far_peers = [(1 - h) * nx + lax.rem(x + i, nx) for i in ring(nx) + [0]]
+    far = (1 - h) * nx + x
     near_peers = [h * nx + lax.rem(x + i, nx) for i in ring(nx)]
-    v_peers = [lax.rem(v + i, nv) for i in range(1, nv)]
+    l_others = [nl - 1 - l] if nl == 2 else [nl - 1 - l, lax.rem(l + 2, 4), l + 1 - 2 * lax.rem(l, 2)]
+    v_peers = [lt * 2 + kt for lt in l_others for kt in (1 - k, k)] + [l * 2 + (1 - k)]
 
     barrier = pltpu.get_barrier_semaphore()
-    for bt in far_peers + near_peers:
+    for bt in [far] + near_peers:
         pl.semaphore_signal(barrier, inc=1, device_id=at(z, bt, v))
     for zt in z_peers:
         pl.semaphore_signal(barrier, inc=1, device_id=at(zt, b, v))
@@ -106,13 +107,13 @@
     loads[2].wait()
     loads[3].wait()
     lg[b] = lat[...]
-    pl.semaphore_wait(barrier, (nz - 1) + (nb - 1) + (nv - 1))
-
-    for bt in far_peers:
-        send(lat, lg.at[b], l_s, l_far, at(z, bt, v))
+    pl.semaphore_wait(barrier, (nz - 1) + nx + (nv - 1))
+
+    facing = at(z, far, v)
+    send(lat, lg.at[b], l_s, l_face, facing)
     for bt in near_peers:
         send(lat, lg.at[b], l_s, l_near, at(z, bt, v))
-    gone(lg.at[pl.ds(0, nb - 1)], l_s)
+    gone(lg.at[pl.ds(0, nx)], l_s)
     mine = pw.at[h, k, z]
     for zt in z_peers:
         send(mine, mine, w_s, w_r, at(zt, b, v))
@@ -124,14 +125,15 @@
         send(ms.at[vt], la.at[v], a_s, a_r, at(z, b, vt))
     gone(ms.at[pl.ds(0, nv - 1)], a_s)
     la[v] = ms[v]
+    came(lat, l_face)
+    for bt in near_peers:
+        send(lg.at[far], lg.at[far], k_s, l_far, at(z, bt, v))
+    gone(lg.at[pl.ds(0, nx - 1)], k_s)
 
     if nz > 1:
         came(pw.at[h, k, pl.ds(0, nz - 1)], w_r)
     neighbour = at(z, b, l * 2 + (1 - k))
-    facing = at(z, (1 - h) * nx + x, v)
     panel = pw.at[h, k]
-    send(panel, panel, p_s.at[0], p_r.at[0], neighbour)
-    gone(panel, p_s.at[0])
     noises = pw[h, k].reshape(wide, depth)
     square = noises.astype(jnp.float32)
     square = jnp.sum(square * square, axis=1, keepdims=True)
@@ -160,7 +162,7 @@
     came(lg.at[pl.ds(0, nx - 1)], l_near)
     block(h)
     r_send(h)
-    came(lg.at[pl.ds(0, nx)], l_far)
+    came(lg.at[pl.ds(0, nx - 1)], l_far)
     block(1 - h)
     r_send(1 - h)
     gone(part.at[pl.ds(0, nv - 1)], r_s)
@@ -192,6 +194,8 @@
     pieces = g.at[pl.ds(0, ny * (nx - 1))]
     gone(pieces, f_s)
     came(pieces, f_r)
+    send(panel, panel, p_s.at[0], p_r.at[0], neighbour)
+    gone(panel, p_s.at[0])
     send(panel, panel, p_s.at[1], p_r.at[1], facing)
     gone(panel, p_s.at[1])
 
@@ -288,8 +292,7 @@
     came(la.at[pl.ds(0, nv - 1)], a_r)
     number = nx * nl
     made = jnp.zeros((rows * st, nv * patches), jnp.float32)
-    for i in range(nl):
-        lt = lax.rem(l + i, nl)
+    for i, lt in enumerate([l] + l_others[::-1]):
         if i == 0:
 
             @pl.when(parity == k)
@@ -335,7 +338,7 @@
     f32, bf16 = jnp.float32, jnp.bfloat16
     vmem = pl.BlockSpec(memory_space=pltpu.VMEM)
     sems = []
-    for shape in (1, 1, 1, 1, 1, 1, 1, 1, 2 * nl, ITERS, ITERS, 1, nl, 1, 1, 3, 3, 4, 1, 1):
+    for shape in (1, 1, 1, 1, 1, 1, 1, 1, 2 * nl, ITERS, ITERS, 1, nl, 1, 1, 3, 3, 4, 1, 1, 1, 1):
         sems.append(pltpu.SemaphoreType.DMA if shape == 1 else pltpu.SemaphoreType.DMA((shape,)))
     tokens = pl.pallas_call(
         functools.partial(couple, nz, nb, nv),

time: 66.6 us -> 65.5 us (0.983)
  Pallas kernels: 64 us -> 63 us
    pallas_call x1, Pallas kernels: 64 us -> 63 us  [on_device(): pl.pallas_call(functools.partial(couple, nz, nb, nv), out_shape=jax.Shape...]
where the time goes in v6:
time: 65.5 us; the launch traced here: 65.3 us
  Pallas kernels  63 us (96%)
  matrix products  2.32 us (4%)
    pallas_call x1, Pallas kernels, on_device(): pl.pallas_call(functools.partial(couple, nz, nb, nv), out_shape=jax.Shape...  63 us
    dot_general x1, matrix products, on_device(): made = jnp.dot(tokens, embed, preferred_element_type=f32).astype(bf16)  2.32 us

profile of v6, /device:TPU:1, one launch (start us, length us, event | category | flops | bytes accessed | tf_op | source)
XLA Modules:
  0.0 65.3 jit_solution(12004811386269669101)
XLA Ops:
  0.0 0.0 copy-start
  0.0 63.0 %couple.1 = bf16[256,64]{1,0:T(8,128)(2,1)S(1)} custom-call(bf16[16,1024]{1,0:T(8,128)(2,1)} %lat_in.1, bf16[16,1024]{1,0:T(8,128)(2,1)} %noise_in.1, s32[4,16]{1,0:T(4,128)} %bitcast.6, f32[16]{0:T(128)} %times_in.1), custom_call_target="tpu_custom_call" | custom-call | tf_op jit(solution)/shard_map/couple/pallas_call | solution.py:343
  63.0 0.0 copy-done
  63.0 2.3 %convolution_convert_fusion = bf16[256,5120]{1,0:T(8,128)(2,1)} fusion(bf16[256,64]{1,0:T(8,128)(2,1)S(1)} %couple.1, bf16[64,5120]{1,0:T(8,128)(2,1)S(1)} %copy-done), kind=kOutput, calls=%fused_computation | convolution fusion | flops 169082880 | bytes 3309568 | tf_op jit(solution)/shard_map/dot_general | solution.py:374
Async XLA Ops:
  0.0 63.0 %copy-start = (bf16[64,5120]{1,0:T(8,128)(2,1)S(1)}, bf16[64,5120]{1,0:T(8,128)(2,1)}, u32[]{:S(2)}) copy-start(bf16[64,5120]{1,0:T(8,128)(2,1)} %param.9) | copy-start | bytes 1966084

commit v7 on v6

--- a/solution.py
+++ b/solution.py
@@ -27,12 +27,11 @@
 
 
 def couple(nz, nb, nv, lat_in, noise_in, off_in, times_in, out, lat, noise, off, times, pw, lg, part, rv, g, ex, urow, pb, rp, ms, la,
-           w_s, w_r, l_s, l_near, l_far, r_s, r_r, g_s, g_r, e_s, e_r, c_s, c_r, a_s, a_r, p_s, p_r, i_s, f_s, f_r, l_face, k_s):
+           w_s, w_r, l_s, l_r, w_far, r_s, r_r, g_s, g_r, e_s, e_r, c_s, c_r, a_s, a_r, p_s, p_r, i_s, f_s, f_r, k_s):
     nl, nx = nv // 2, nb // 2
     rows, depth = lat.shape
     patches = depth // S
-    wide = nz * rows
-    n = nb * wide
+    wide = nb * rows
     st = S // nv
     width = patches * rows
     clip = lax.axis_index("clip")
@@ -40,7 +39,9 @@
     z, b = clip // nb, lax.rem(clip, nb)
     h, x = b // nx, lax.rem(b, nx)
     l, k = v // 2, lax.rem(v, 2)
-    y = h * nl + l
+    y, ny = h * nl + l, 2 * nl
+    nh = nz // 2
+    zh, zl = z // nh, lax.rem(z, nh)
     left = []
 
     def at(z_, b_, v_):
@@ -103,38 +104,37 @@
                 row >= bit, pltpu.roll(t, bit * GW, 1), pltpu.roll(t, S - GH * GW + bit * GW, 1)
             )
             t = jnp.where((sy & bit) != 0, turned, t)
-        pw[h, k, z, :, p * S:(p + 1) * S] = t.astype(jnp.bfloat16)
+        pw[zh, k, b, :, p * S:(p + 1) * S] = t.astype(jnp.bfloat16)
     loads[2].wait()
     loads[3].wait()
-    lg[b] = lat[...]
+    lg[z] = lat[...]
     pl.semaphore_wait(barrier, (nz - 1) + nx + (nv - 1))
 
-    facing = at(z, far, v)
-    send(lat, lg.at[b], l_s, l_face, facing)
+    for zt in z_peers:
+        send(lat, lg.at[z], l_s, l_r, at(zt, b, v))
+    gone(lg.at[pl.ds(0, nz - 1)], l_s)
+    mine = pw.at[zh, k, b]
+    send(mine, mine, w_s, w_far, at(z, far, v))
     for bt in near_peers:
-        send(lat, lg.at[b], l_s, l_near, at(z, bt, v))
-    gone(lg.at[pl.ds(0, nx)], l_s)
-    mine = pw.at[h, k, z]
-    for zt in z_peers:
-        send(mine, mine, w_s, w_r, at(zt, b, v))
-    if nz > 1:
-        gone(pw.at[h, k, pl.ds(0, nz - 1)], w_s)
+        send(mine, mine, w_s, w_r, at(z, bt, v))
+    gone(pw.at[zh, k, pl.ds(0, nx)], w_s)
 
     ms[...] = turn(lat[...].astype(jnp.float32), patches).astype(jnp.bfloat16).reshape(nv, st, width)
     for vt in v_peers:
         send(ms.at[vt], la.at[v], a_s, a_r, at(z, b, vt))
     gone(ms.at[pl.ds(0, nv - 1)], a_s)
     la[v] = ms[v]
-    came(lat, l_face)
+    came(mine, w_far)
+    passed = pw.at[zh, k, far]
     for bt in near_peers:
-        send(lg.at[far], lg.at[far], k_s, l_far, at(z, bt, v))
-    gone(lg.at[pl.ds(0, nx - 1)], k_s)
-
-    if nz > 1:
-        came(pw.at[h, k, pl.ds(0, nz - 1)], w_r)
+        send(passed, passed, k_s, w_r, at(z, bt, v))
+    gone(pw.at[zh, k, pl.ds(0, nx - 1)], k_s)
+    came(lg.at[pl.ds(0, nz - 1)], l_r)
+    came(pw.at[zh, k, pl.ds(0, 2 * (nx - 1))], w_r)
     neighbour = at(z, b, l * 2 + (1 - k))
-    panel = pw.at[h, k]
-    noises = pw[h, k].reshape(wide, depth)
+    facing = at(lax.rem(z + nh, nz), b, v)
+    panel = pw.at[zh, k]
+    noises = pw[zh, k].reshape(wide, depth)
     square = noises.astype(jnp.float32)
     square = jnp.sum(square * square, axis=1, keepdims=True)
     diagonal = lax.broadcasted_iota(jnp.int32, (wide, wide), 0) == lax.broadcasted_iota(
@@ -142,56 +142,40 @@
     )
     square = jnp.sum(jnp.where(diagonal, square, 0.0), axis=0, keepdims=True)
 
-    def block(half):
-        gram = lax.dot_general(
-            lg[pl.ds(half * nx, nx)].reshape(nx * rows, depth),
-            pw[h, k].reshape(wide, depth),
-            (((1,), (1,)), ((), ())),
-            preferred_element_type=jnp.float32,
-        )
-        part[pl.ds(half * nx, nx)] = (square - 2.0 * gram).reshape(nx, rows, wide)
-
-    def r_send(half):
-        for i in range(nx):
-            vt = half * nx + lax.rem(x + i, nx)
-
-            @pl.when(vt != v)
-            def _():
-                send(part.at[vt], rv.at[v], r_s, r_r, at(z, b, vt))
-
-    came(lg.at[pl.ds(0, nx - 1)], l_near)
-    block(h)
-    r_send(h)
-    came(lg.at[pl.ds(0, nx - 1)], l_far)
-    block(1 - h)
-    r_send(1 - h)
+    gram = lax.dot_general(
+        lg[...].reshape(nz * rows, depth), noises, (((1,), (1,)), ((), ())), preferred_element_type=jnp.float32
+    )
+    part[...] = (square - 2.0 * gram).reshape(nz, rows, wide)
+    for vt in v_peers:
+        send(part.at[vt], rv.at[v], r_s, r_r, at(z, b, vt))
     gone(part.at[pl.ds(0, nv - 1)], r_s)
     rv[v] = part[v]
     came(rv.at[pl.ds(0, nv - 1)], r_r)
     volume = float(nv * depth)
     entropy = 0.5 / math.sqrt(volume)
 
-    piece = g.at[b * nl + l]
+    piece = g.at[z * ny + y]
     piece[...] = jnp.sum(rv[...], axis=0) * (LOG2E / (volume * entropy))
 
-    ny = 2 * nl
-    x_peers = [lax.rem(x + i, nx) for i in ring(nx)]
-
-    def pass_on(h_, l_):
-        here = g.at[(h_ * nx + x) * nl + l_]
-        for xt in x_peers:
-            send(here, here, f_s, f_r, at(z, h * nx + xt, v))
-
-    for i in ring(ny):
-        yt = lax.rem(y + i, ny)
-        send(piece, piece, g_s, g_r.at[i], at(z, yt // nl * nx + x, lax.rem(yt, nl) * 2 + k))
-    pass_on(h, l)
-    for i in reversed(ring(ny)):
-        yt = lax.rem(y + ny - i, ny)
-        came(piece, g_r.at[i])
-        pass_on(yt // nl, lax.rem(yt, nl))
-    gone(g.at[pl.ds(0, ny - 1)], g_s)
-    pieces = g.at[pl.ds(0, ny * (nx - 1))]
+    def at_y(i):
+        return at(z, i // nl * nx + x, lax.rem(i, nl) * 2 + k)
+
+    y_peers = [lax.rem(y + i, ny) for i in ring(ny)]
+    for i, yt, zt in zip(ring(nz), y_peers, z_peers):
+        send(piece, piece, g_s, g_r.at[0, i], at_y(yt))
+        send(piece, piece, g_s, g_r.at[1, i], at(zt, b, v))
+    gone(g.at[pl.ds(0, ny - 1 + nz - 1)], g_s)
+    for i in reversed(ring(nz)):
+        yt, zt = lax.rem(y + ny - i, ny), lax.rem(z + nz - i, nz)
+        came(piece, g_r.at[0, i])
+        part_of = g.at[z * ny + yt, pl.ds(0, rows // 2)]
+        for onward in z_peers:
+            send(part_of, part_of, f_s, f_r, at(onward, b, v))
+        came(piece, g_r.at[1, i])
+        part_of = g.at[zt * ny + y, pl.ds(rows // 2, rows // 2)]
+        for onward in y_peers:
+            send(part_of, part_of, f_s, f_r, at_y(onward))
+    pieces = g.at[pl.ds(0, (ny - 1) * (nz - 1))]
     gone(pieces, f_s)
     came(pieces, f_r)
     send(panel, panel, p_s.at[0], p_r.at[0], neighbour)
@@ -199,13 +183,13 @@
     send(panel, panel, p_s.at[1], p_r.at[1], facing)
     gone(panel, p_s.at[1])
 
-    blocks = nb
-    own_e = z * 2 + k
-
-    def tile(c, first=0, count=nl):
-        return g[pl.ds(c * nl + first, count)].reshape(count * rows, wide)
-
-    def row_stats(dual, first=0, count=nl):
+    blocks = nz
+    own_e = x * 2 + k
+
+    def tile(c, first=0, count=ny):
+        return g[pl.ds(c * ny + first, count)].reshape(count * rows, wide)
+
+    def row_stats(dual, first=0, count=ny):
         top = dual[0:1] - tile(0, first, count)
         for c in range(1, blocks):
             top = jnp.maximum(top, dual[c:c + 1] - tile(c, first, count))
@@ -215,7 +199,7 @@
             total = total + jnp.exp2(dual[c:c + 1] - tile(c, first, count) - top)
         return top, jnp.sum(total, axis=1, keepdims=True)
 
-    e_peers = [(z_, q) for z_ in z_peers for q in (1 - k, k)] + [(z, 1 - k)]
+    e_peers = [(bt, kt) for bt in near_peers for kt in (1 - k, k)] + [(b, 1 - k)]
 
     dual = jnp.zeros((blocks, wide), jnp.float32)
     for it in range(ITERS):
@@ -228,12 +212,12 @@
             ex[it, own_e, c:c + 1] = top + jnp.log2(total)
         here = ex.at[it, own_e]
 
-        for zt, kt in e_peers:
-            send(here, here, e_s.at[it], e_r.at[it], at(zt, b, l * 2 + kt))
-        others = ex.at[it, pl.ds(0, 2 * nz - 1)]
+        for bt, kt in e_peers:
+            send(here, here, e_s.at[it], e_r.at[it], at(z, bt, l * 2 + kt))
+        others = ex.at[it, pl.ds(0, 2 * nx - 1)]
         gone(others, e_s.at[it])
         if it == ITERS - 1:
-            passed = pw.at[1 - h, k]
+            passed = pw.at[1 - zh, k]
             came(passed, p_r.at[1])
             send(passed, passed, p_s.at[2], p_r.at[2], neighbour)
             gone(passed, p_s.at[2])
@@ -245,18 +229,18 @@
 
     urow[...] = dual
     count = nl // 2
-    start = h * count
+    start = h * nl + zh * count
     top, total = row_stats(dual, start, count)
     weights = []
     for half in range(2):
-        at_x = half * nx + x
-        t = urow[pl.ds(at_x, 1)] - g[pl.ds(at_x * nl + start, count)].reshape(count * rows, wide)
+        at_z = half * nh + zl
+        t = urow[pl.ds(at_z, 1)] - g[pl.ds(at_z * ny + start, count)].reshape(count * rows, wide)
         weights.append((jnp.exp2(t - top) / total).astype(jnp.bfloat16))
 
-    came(pw.at[h, 1 - k], p_r.at[0])
-    came(pw.at[1 - h, 1 - k], p_r.at[2])
-    parity = lax.rem(x, 2)
-    slot = l * nx + x
+    came(pw.at[zh, 1 - k], p_r.at[0])
+    came(pw.at[1 - zh, 1 - k], p_r.at[2])
+    parity = lax.rem(zl, 2)
+    slot = l * nh + zl
     partial = []
     for kk in range(2):
         coupled = jnp.dot(weights[0], pw[0, kk].reshape(wide, depth), preferred_element_type=jnp.float32)
@@ -268,17 +252,17 @@
         for kk in range(2):
             made = turn(partial[kk][i * rows:(i + 1) * rows], patches).astype(jnp.bfloat16)
             pb[i * nv:(i + 1) * nv, kk] = made.reshape(nv, st, width)
-        xt = 2 * i + k
+        zt = 2 * i + k
         for vt in v_peers:
-            send(pb.at[i * nv + vt], rp.at[slot], c_s, c_r.at[l], at(z, h * nx + xt, vt))
-
-        @pl.when(xt != x)
+            send(pb.at[i * nv + vt], rp.at[slot], c_s, c_r.at[l], at(zh * nh + zt, b, vt))
+
+        @pl.when(zt != zl)
         def _():
-            send(pb.at[i * nv + v], rp.at[slot], c_s, c_r.at[l], at(z, h * nx + xt, v))
+            send(pb.at[i * nv + v], rp.at[slot], c_s, c_r.at[l], at(zh * nh + zt, b, v))
 
     @pl.when(parity == k)
     def _():
-        rp[slot] = pb[x // 2 * nv + v]
+        rp[slot] = pb[zl // 2 * nv + v]
 
     finish()
     lane = lax.broadcasted_iota(jnp.int32, (st, width), 1) & (rows - 1)
@@ -290,25 +274,25 @@
     from_lane = lax.broadcasted_iota(jnp.int32, (width, nv * patches), 0) // rows
     to_patch = lax.broadcasted_iota(jnp.int32, (width, nv * patches), 1)
     came(la.at[pl.ds(0, nv - 1)], a_r)
-    number = nx * nl
+    number = nh * nl
     made = jnp.zeros((rows * st, nv * patches), jnp.float32)
     for i, lt in enumerate([l] + l_others[::-1]):
         if i == 0:
 
             @pl.when(parity == k)
             def _():
-                came(rp.at[pl.ds(0, nx - 1)], c_r.at[lt])
+                came(rp.at[pl.ds(0, nh - 1)], c_r.at[lt])
 
             @pl.when(parity != k)
             def _():
-                came(rp.at[pl.ds(0, nx)], c_r.at[lt])
+                came(rp.at[pl.ds(0, nh)], c_r.at[lt])
 
         else:
-            came(rp.at[pl.ds(0, nx)], c_r.at[lt])
+            came(rp.at[pl.ds(0, nh)], c_r.at[lt])
         for kk in range(2):
-            coupled = rp[lt * nx, kk].astype(jnp.float32)
-            for xt in range(1, nx):
-                coupled = coupled + rp[lt * nx + xt, kk].astype(jnp.float32)
+            coupled = rp[lt * nh, kk].astype(jnp.float32)
+            for zt in range(1, nh):
+                coupled = coupled + rp[lt * nh + zt, kk].astype(jnp.float32)
             mixed = (1.0 - time) * la[lt * 2 + kk].astype(jnp.float32) + time * coupled
             spread = jnp.where(keep, mixed[None], 0.0).reshape(rows * st, width).astype(jnp.bfloat16)
             start = (lt * 2 + kk) * patches
@@ -333,13 +317,14 @@
     rows, depth = latents.shape
     patches = depth // S
     st = S // nv
-    wide = nz * rows
+    nh = nz // 2
+    wide = nb * rows
     width = patches * rows
     f32, bf16 = jnp.float32, jnp.bfloat16
     vmem = pl.BlockSpec(memory_space=pltpu.VMEM)
     sems = []
-    for shape in (1, 1, 1, 1, 1, 1, 1, 1, 2 * nl, ITERS, ITERS, 1, nl, 1, 1, 3, 3, 4, 1, 1, 1, 1):
-        sems.append(pltpu.SemaphoreType.DMA if shape == 1 else pltpu.SemaphoreType.DMA((shape,)))
+    for shape in ((), (), (), (), (), (), (), (), (2, nz), (ITERS,), (ITERS,), (), (nl,), (), (), (3,), (3,), (4,), (), (), ()):
+        sems.append(pltpu.SemaphoreType.DMA(shape) if shape else pltpu.SemaphoreType.DMA)
     tokens = pl.pallas_call(
         functools.partial(couple, nz, nb, nv),
         out_shape=jax.ShapeDtypeStruct((rows * st, nv * patches), bf16),
@@ -350,15 +335,15 @@
             pltpu.VMEM((rows, depth), bf16),
             pltpu.SMEM((4, rows), jnp.int32),
             pltpu.SMEM((rows,), f32),
-            pltpu.VMEM((2, 2, nz, rows, depth), bf16),
-            pltpu.VMEM((nb, rows, depth), bf16),
-            pltpu.VMEM((nb, rows, wide), f32),
+            pltpu.VMEM((2, 2, nb, rows, depth), bf16),
+            pltpu.VMEM((nz, rows, depth), bf16),
+            pltpu.VMEM((nz, rows, wide), f32),
             pltpu.VMEM((nv, rows, wide), f32),
-            pltpu.VMEM((nb * nl, rows, wide), f32),
-            pltpu.VMEM((ITERS, 2 * nz, nb, wide), f32),
-            pltpu.VMEM((nb, wide), f32),
+            pltpu.VMEM((nz * 2 * nl, rows, wide), f32),
+            pltpu.VMEM((ITERS, 2 * nx, nz, wide), f32),
+            pltpu.VMEM((nz, wide), f32),
             pltpu.VMEM((nl // 2 * nv, 2, st, width), bf16),
-            pltpu.VMEM((nx * nl, 2, st, width), bf16),
+            pltpu.VMEM((nh * nl, 2, st, width), bf16),
             pltpu.VMEM((nv, st, width), bf16),
             pltpu.VMEM((nv, st, width), bf16),
             *sems,

time: 65.5 us -> 63.6 us (0.971)
  Pallas kernels: 63 us -> 61.1 us
    pallas_call x1, Pallas kernels: 63 us -> 61.1 us  [on_device(): pl.pallas_call(functools.partial(couple, nz, nb, nv), out_shape=jax.Shape...]
where the time goes in v7:
time: 63.6 us; the launch traced here: 63.5 us
  Pallas kernels  61.1 us (96%)
  matrix products  2.32 us (4%)
    pallas_call x1, Pallas kernels, on_device(): pl.pallas_call(functools.partial(couple, nz, nb, nv), out_shape=jax.Shape...  61.1 us
    dot_general x1, matrix products, on_device(): made = jnp.dot(tokens, embed, preferred_element_type=f32).astype(bf16)  2.32 us

profile of v7, /device:TPU:1, one launch (start us, length us, event | category | flops | bytes accessed | tf_op | source)
XLA Modules:
  0.0 63.5 jit_solution(10247713055759747264)
XLA Ops:
  0.0 0.0 copy-start
  0.0 61.1 %couple.1 = bf16[256,64]{1,0:T(8,128)(2,1)S(1)} custom-call(bf16[16,1024]{1,0:T(8,128)(2,1)} %lat_in.1, bf16[16,1024]{1,0:T(8,128)(2,1)} %noise_in.1, s32[4,16]{1,0:T(4,128)} %bitcast.6, f32[16]{0:T(128)} %times_in.1), custom_call_target="tpu_custom_call" | custom-call | tf_op jit(solution)/shard_map/couple/pallas_call | solution.py:328
  61.1 0.0 copy-done
  61.2 2.3 %convolution_convert_fusion = bf16[256,5120]{1,0:T(8,128)(2,1)} fusion(bf16[256,64]{1,0:T(8,128)(2,1)S(1)} %couple.1, bf16[64,5120]{1,0:T(8,128)(2,1)S(1)} %copy-done), kind=kOutput, calls=%fused_computation | convolution fusion | flops 169082880 | bytes 3309568 | tf_op jit(solution)/shard_map/dot_general | solution.py:359
Async XLA Ops:
  0.0 61.1 %copy-start = (bf16[64,5120]{1,0:T(8,128)(2,1)S(1)}, bf16[64,5120]{1,0:T(8,128)(2,1)}, u32[]{:S(2)}) copy-start(bf16[64,5120]{1,0:T(8,128)(2,1)} %param.9) | copy-start | bytes 1966084

commit v8 on v7

--- a/solution.py
+++ b/solution.py
@@ -168,13 +168,15 @@
     for i in reversed(ring(nz)):
         yt, zt = lax.rem(y + ny - i, ny), lax.rem(z + nz - i, nz)
         came(piece, g_r.at[0, i])
-        part_of = g.at[z * ny + yt, pl.ds(0, rows // 2)]
-        for onward in z_peers:
-            send(part_of, part_of, f_s, f_r, at(onward, b, v))
+        whole = g.at[z * ny + yt]
+        for j, onward in zip(ring(nz), z_peers):
+            if (i + j) % 2 == 0:
+                send(whole, whole, f_s, f_r, at(onward, b, v))
         came(piece, g_r.at[1, i])
-        part_of = g.at[zt * ny + y, pl.ds(rows // 2, rows // 2)]
-        for onward in y_peers:
-            send(part_of, part_of, f_s, f_r, at_y(onward))
+        whole = g.at[zt * ny + y]
+        for j, onward in zip(ring(ny), y_peers):
+            if (i + j) % 2:
+                send(whole, whole, f_s, f_r, at_y(onward))
     pieces = g.at[pl.ds(0, (ny - 1) * (nz - 1))]
     gone(pieces, f_s)
     came(pieces, f_r)

time: 63.6 us -> 63.3 us (level)
  no operation moved by 1% of the time
where the time goes in v8:
time: 63.3 us; the launch traced here: 63.1 us
  Pallas kernels  60.8 us (96%)
  matrix products  2.32 us (4%)
    pallas_call x1, Pallas kernels, on_device(): pl.pallas_call(functools.partial(couple, nz, nb, nv), out_shape=jax.Shape...  60.8 us
    dot_general x1, matrix products, on_device(): made = jnp.dot(tokens, embed, preferred_element_type=f32).astype(bf16)  2.32 us

profile of v8, /device:TPU:1, one launch (start us, length us, event | category | flops | bytes accessed | tf_op | source)
XLA Modules:
  0.0 63.1 jit_solution(3607826149297663314)
XLA Ops:
  0.0 0.0 copy-start
  0.0 60.8 %couple.1 = bf16[256,64]{1,0:T(8,128)(2,1)S(1)} custom-call(bf16[16,1024]{1,0:T(8,128)(2,1)} %lat_in.1, bf16[16,1024]{1,0:T(8,128)(2,1)} %noise_in.1, s32[4,16]{1,0:T(4,128)} %bitcast.6, f32[16]{0:T(128)} %times_in.1), custom_call_target="tpu_custom_call" | custom-call | tf_op jit(solution)/shard_map/couple/pallas_call | solution.py:330
  60.8 0.0 copy-done
  60.8 2.3 %convolution_convert_fusion = bf16[256,5120]{1,0:T(8,128)(2,1)} fusion(bf16[256,64]{1,0:T(8,128)(2,1)S(1)} %couple.1, bf16[64,5120]{1,0:T(8,128)(2,1)S(1)} %copy-done), kind=kOutput, calls=%fused_computation | convolution fusion | flops 169082880 | bytes 3309568 | tf_op jit(solution)/shard_map/dot_general | solution.py:361
Async XLA Ops:
  0.0 60.8 %copy-start = (bf16[64,5120]{1,0:T(8,128)(2,1)S(1)}, bf16[64,5120]{1,0:T(8,128)(2,1)}, u32[]{:S(2)}) copy-start(bf16[64,5120]{1,0:T(8,128)(2,1)} %param.9) | copy-start | bytes 1966084

commit v9 on v8

--- a/solution.py
+++ b/solution.py
@@ -20,6 +20,11 @@
 
 def ring(n):
     return sorted(range(1, n), key=lambda i: -min(i, n - i))
+
+
+def along_y_first(i, j, n):
+    by_y, by_z = min(i, n - i), min(j, n - j)
+    return by_y > by_z or (by_y == by_z and (i + j) % n == 0)
 
 
 def turn(x, patches):
@@ -110,14 +115,14 @@
     lg[z] = lat[...]
     pl.semaphore_wait(barrier, (nz - 1) + nx + (nv - 1))
 
-    for zt in z_peers:
-        send(lat, lg.at[z], l_s, l_r, at(zt, b, v))
-    gone(lg.at[pl.ds(0, nz - 1)], l_s)
     mine = pw.at[zh, k, b]
     send(mine, mine, w_s, w_far, at(z, far, v))
     for bt in near_peers:
         send(mine, mine, w_s, w_r, at(z, bt, v))
     gone(pw.at[zh, k, pl.ds(0, nx)], w_s)
+    for zt in z_peers:
+        send(lat, lg.at[z], l_s, l_r, at(zt, b, v))
+    gone(lg.at[pl.ds(0, nz - 1)], l_s)
 
     ms[...] = turn(lat[...].astype(jnp.float32), patches).astype(jnp.bfloat16).reshape(nv, st, width)
     for vt in v_peers:
@@ -170,12 +175,12 @@
         came(piece, g_r.at[0, i])
         whole = g.at[z * ny + yt]
         for j, onward in zip(ring(nz), z_peers):
-            if (i + j) % 2 == 0:
+            if along_y_first(i, j, ny):
                 send(whole, whole, f_s, f_r, at(onward, b, v))
         came(piece, g_r.at[1, i])
         whole = g.at[zt * ny + y]
         for j, onward in zip(ring(ny), y_peers):
-            if (i + j) % 2:
+            if not along_y_first(j, i, ny):
                 send(whole, whole, f_s, f_r, at_y(onward))
     pieces = g.at[pl.ds(0, (ny - 1) * (nz - 1))]
     gone(pieces, f_s)

time: 63.3 us -> 63 us (level)
  no operation moved by 1% of the time
where the time goes in v9:
time: 63 us; the launch traced here: 62.9 us
  Pallas kernels  60.5 us (96%)
  matrix products  2.32 us (4%)
    pallas_call x1, Pallas kernels, on_device(): pl.pallas_call(functools.partial(couple, nz, nb, nv), out_shape=jax.Shape...  60.5 us
    dot_general x1, matrix products, on_device(): made = jnp.dot(tokens, embed, preferred_element_type=f32).astype(bf16)  2.32 us

profile of v9, /device:TPU:1, one launch (start us, length us, event | category | flops | bytes accessed | tf_op | source)
XLA Modules:
  0.0 62.9 jit_solution(14355547490797229504)
XLA Ops:
  0.0 0.0 copy-start
  0.0 60.5 %couple.1 = bf16[256,64]{1,0:T(8,128)(2,1)S(1)} custom-call(bf16[16,1024]{1,0:T(8,128)(2,1)} %lat_in.1, bf16[16,1024]{1,0:T(8,128)(2,1)} %noise_in.1, s32[4,16]{1,0:T(4,128)} %bitcast.6, f32[16]{0:T(128)} %times_in.1), custom_call_target="tpu_custom_call" | custom-call | tf_op jit(solution)/shard_map/couple/pallas_call | solution.py:335
  60.6 0.0 copy-done
  60.6 2.3 %convolution_convert_fusion = bf16[256,5120]{1,0:T(8,128)(2,1)} fusion(bf16[256,64]{1,0:T(8,128)(2,1)S(1)} %couple.1, bf16[64,5120]{1,0:T(8,128)(2,1)S(1)} %copy-done), kind=kOutput, calls=%fused_computation | convolution fusion | flops 169082880 | bytes 3309568 | tf_op jit(solution)/shard_map/dot_general | solution.py:366
Async XLA Ops:
  0.0 60.6 %copy-start = (bf16[64,5120]{1,0:T(8,128)(2,1)S(1)}, bf16[64,5120]{1,0:T(8,128)(2,1)}, u32[]{:S(2)}) copy-start(bf16[64,5120]{1,0:T(8,128)(2,1)} %param.9) | copy-start | bytes 1966084
